TPU v7x, 512 devices: a whole 4x8x8 slice. The times are simulated.
512 devices in a mesh: dp: 32 (over z, x), param: 16 (over y, core).
Axes of the slice: x: 4, y: 8, z: 8, core: 2. Of those that a mesh axis runs over, the one named last changes fastest.
Arguments:
- features: bfloat16 [32768, 2048], P('dp'), may hold values from -24 to 24
- w_hidden: bfloat16 [2048, 2048], P(None, 'param'), may hold values from -0.125 to 0.125
- w_head: bfloat16 [2048, 36], P('param'), may hold values from -0.03125 to 0.03125
- base_mean: float32 [32768, 36], P('dp'), may hold values from -5 to 5
- actions: float32 [32768, 36], P('dp'), may hold values from -7 to 7
- advantages: float32 [32768], P('dp'), may hold values from -4 to 4
- log_std: float32 [36], replicated, may hold values from -1 to 0
Outputs:
- step_unit: float32 [2048, 2048], P('dp', 'param')
- kl_ratio: float32 [], replicated
All inputs are finite; a program needn't handle non-finite values.
Results may differ from a plain program's by a relative error of at most 0.0049.
Values may be sent and summed in bfloat16 or wider, within the bound.
A program may use at most 64 MiB of HBM per device.

v0:
```python
import jax
import jax.numpy as jnp
from jax import lax
from jax.sharding import PartitionSpec as P

D = 2048
UNITS = 2048
ITERS = 2


DAMPING = 0.01
TRIAL_KL = 4.0


def shards(features, w_hidden, w_head, base_mean, actions, advantages, log_std):
    highest = lax.Precision.HIGHEST
    rows = features.shape[0]
    width = features.shape[1]
    dp_count = lax.axis_size("dp")
    batch = rows * dp_count
    inv_var = jnp.exp(-2.0 * log_std)
    pre = jnp.dot(features, w_hidden, preferred_element_type=jnp.float32)
    hidden = jnp.tanh(pre)
    slope = 1.0 - hidden * hidden

    def head_total(part):
        return lax.psum(jnp.dot(part, w_head, preferred_element_type=jnp.float32), "param")

    mean = base_mean + head_total(hidden.astype(jnp.bfloat16))
    delta = advantages[:, None] * (actions - mean) * inv_var
    head_t = w_head.astype(jnp.float32).T

    def pull(moment):
        return (jnp.dot(moment, head_t, precision=highest) * slope / batch).astype(jnp.bfloat16)

    def rowsum(grads):
        term = lax.dot_general(
            features, grads, (((0,), (0,)), ((), ())), preferred_element_type=jnp.float32
        )
        return lax.psum(term, "dp")

    def expand(vector_b):
        return jnp.dot(features, vector_b, preferred_element_type=jnp.float32)

    def total(values):
        return lax.psum((values[0],), "param")

    grad = rowsum(pull(delta))
    solution = jnp.zeros_like(grad)
    resid = grad
    direction = grad
    (norm_now,) = total((jnp.sum(resid * resid),))
    for turn in range(ITERS):
        change = expand(direction.astype(jnp.bfloat16))
        dmu = head_total((change * slope).astype(jnp.bfloat16))
        image = rowsum(pull(dmu * inv_var)) + DAMPING * direction
        image, dmu = (image, dmu)
        (curv,) = total((jnp.sum(direction * image),))
        alpha = norm_now / curv
        solution = solution + alpha * direction
        resid = resid - alpha * image
        (norm_next,) = total((jnp.sum(resid * resid),))
        direction = resid + norm_next / norm_now * direction
        norm_now = norm_next
    (shs,) = total((jnp.sum(solution * (grad - resid)),))
    block = width // dp_count
    step_unit = lax.dynamic_slice_in_dim(
        solution * jnp.sqrt(D * UNITS / shs), lax.axis_index("dp") * block, block, 0
    )
    reach = jnp.sqrt(2.0 * TRIAL_KL / shs)
    moved = expand((reach * solution).astype(jnp.bfloat16))
    shift = (jnp.tanh(pre + moved) - hidden).astype(jnp.bfloat16)
    dmean = head_total(shift)
    kl_value = lax.psum(jnp.sum(dmean * dmean * inv_var) / (2.0 * batch), "dp")
    return (step_unit, kl_value / TRIAL_KL)


def solution(mesh):
    return jax.shard_map(
        shards,
        mesh=mesh,
        in_specs=(
            P("dp", None),
            P(None, "param"),
            P("param", None),
            P("dp", None),
            P("dp", None),
            P("dp"),
            P(),
        ),
        out_specs=(P("dp", "param"), P()),
        check_vma=False,
    )
```

profile of v0, /device:TPU:1, one launch (start us, length us, event | category | flops | bytes accessed | tf_op | source)
XLA Modules:
  0.0 1137.9 jit_solution(4026722061031804049)
XLA Ops:
  7.2 0.0 copy-start
  7.2 0.0 copy-start.3
  7.2 0.0 copy-start.7
  7.2 0.0 copy-start.5
  7.2 0.0 copy-start.4
  7.2 0.0 copy-start.6
  7.2 0.0 all-reduce.9.cloned.1.call-start
  7.3 0.9 copy-done
  8.2 3.4 fusion.42
  11.6 0.0 copy-done.3
  11.7 0.9 fusion.27
  12.6 0.0 all-reduce.9.cloned.1.call-update
  12.6 0.0 all-reduce.11.cloned.1.call-start
  12.7 0.0 copy-done.7
  12.7 113.8 %all-reduce.9.cloned.1.call-done = f32[1024,36]{0,1:T(8,128)} async-done(((f32[1024,36]{0,1:T(8,128)}), f32[1024,36]{0,1:T(8,128)}) %all-reduce.9.cloned.1.call-update) | async-done | bytes 147472 | tf_op jit(solution)/shard_map/psum | solution.py:27
  126.5 0.0 copy-done.5
  126.5 0.0 copy-done.4
  126.5 0.0 copy-done.6
  126.5 1.6 fusion.11
  128.1 4.0 convolution_bitcast_fusion.2
  132.1 0.0 all-reduce.11.cloned.1.call-update
  132.1 0.0 all-reduce.13.cloned.1.call-start
  132.2 155.4 %all-reduce.11.cloned.1.call-done = f32[2048,128]{0,1:T(8,128)} async-done(((f32[2048,128]{0,1:T(8,128)}), f32[2048,128]{0,1:T(8,128)}) %all-reduce.11.cloned.1.call-update) | async-done | bytes 1048592 | tf_op jit(solution)/shard_map/psum | solution.py:40
  287.6 4.7 fusion.16
  292.3 0.0 copy-start.1
  292.3 0.0 all-reduce.13.cloned.1.call-update
  292.3 0.0 all-reduce.15.cloned.1.call-start
  292.3 110.0 %all-reduce.13.cloned.1.call-done = f32[1024,36]{0,1:T(8,128)} async-done(((f32[1024,36]{0,1:T(8,128)}), f32[1024,36]{0,1:T(8,128)}) %all-reduce.13.cloned.1.call-update) | async-done | bytes 147472 | tf_op jit(solution)/shard_map/psum | solution.py:27
  402.4 1.6 fusion.10
  404.0 3.9 convolution_bitcast_fusion.1
  407.9 0.0 all-reduce.15.cloned.1.call-update
  407.9 0.0 all-reduce.17.cloned.1.call-start
  408.0 155.4 %all-reduce.15.cloned.1.call-done = f32[2048,128]{0,1:T(8,128)} async-done(((f32[2048,128]{0,1:T(8,128)}), f32[2048,128]{0,1:T(8,128)}) %all-reduce.15.cloned.1.call-update) | async-done | bytes 1048592 | tf_op jit(solution)/shard_map/psum | solution.py:40
  563.4 0.0 copy-done.1
  563.4 0.0 copy-start.2
  563.4 2.2 multiply_reduce_fusion.3
  565.6 28.7 %all-reduce = (f32[]{:T(128)}, f32[]{:T(128)}) all-reduce(f32[]{:T(128)} %get-tuple-element.5, f32[]{:T(128)} %get-tuple-element.4), channel_id=1, replica_groups=mesh['dp'=32,'param'=16] {'param'}, use_global_device_ids=true, to_apply=%region_3.0 | all-reduce | flops 2 | bytes 16 | tf_op jit(solution)/shard_map/psum | solution.py:46
  595.7 2.1 multiply_reduce_fusion.2
  597.8 24.2 %psum.97 = f32[]{:T(128)} all-reduce(f32[]{:T(128)} %multiply_reduce_fusion.2), channel_id=1, replica_groups=mesh['dp'=32,'param'=16] {'param'}, use_global_device_ids=true, to_apply=%region_9.0 | all-reduce | flops 1 | bytes 8 | tf_op jit(solution)/shard_map/psum | solution.py:46
  623.3 0.0 copy-done.2
  623.3 4.4 fusion.15
  627.6 0.0 all-reduce.17.cloned.1.call-update
  627.7 0.0 all-reduce.19.cloned.1.call-start
  627.7 105.3 %all-reduce.17.cloned.1.call-done = f32[1024,36]{0,1:T(8,128)} async-done(((f32[1024,36]{0,1:T(8,128)}), f32[1024,36]{0,1:T(8,128)}) %all-reduce.17.cloned.1.call-update) | async-done | bytes 147472 | tf_op jit(solution)/shard_map/psum | solution.py:27
  733.0 1.6 fusion.9
  734.6 3.9 convolution_bitcast_fusion
  738.5 0.0 all-reduce.19.cloned.1.call-update
  738.5 0.0 all-reduce.21.cloned.1.call-start
  738.6 155.4 %all-reduce.19.cloned.1.call-done = f32[2048,128]{0,1:T(8,128)} async-done(((f32[2048,128]{0,1:T(8,128)}), f32[2048,128]{0,1:T(8,128)}) %all-reduce.19.cloned.1.call-update) | async-done | bytes 1048592 | tf_op jit(solution)/shard_map/psum | solution.py:40
  894.0 2.2 multiply_reduce_fusion.1
  896.2 28.7 %psum.100 = f32[]{:T(128)} all-reduce(f32[]{:T(128)} %multiply_reduce_fusion.1), channel_id=1, replica_groups=mesh['dp'=32,'param'=16] {'param'}, use_global_device_ids=true, to_apply=%region_13.0 | all-reduce | flops 1 | bytes 8 | tf_op jit(solution)/shard_map/psum | solution.py:46
  926.2 3.4 multiply_reduce_fusion
  929.6 24.2 %psum.101 = f32[]{:T(128)} all-reduce(f32[]{:T(128)} %get-tuple-element.8), channel_id=1, replica_groups=mesh['dp'=32,'param'=16] {'param'}, use_global_device_ids=true, to_apply=%region_15.0 | all-reduce | flops 1 | bytes 8 | tf_op jit(solution)/shard_map/psum | solution.py:46
  954.5 4.6 fusion.14
  959.0 0.0 all-reduce.21.cloned.1.call-update
  959.8 0.9 dynamic-slice_multiply_fusion
  960.7 103.7 %all-reduce.21.cloned.1.call-done = f32[1024,36]{0,1:T(8,128)} async-done(((f32[1024,36]{0,1:T(8,128)}), f32[1024,36]{0,1:T(8,128)}) %all-reduce.21.cloned.1.call-update) | async-done | bytes 147472 | tf_op jit(solution)/shard_map/psum | solution.py:27
  1064.5 1.6 multiply_reduce_fusion.5
  1066.7 0.7 copy.9
  1067.4 61.9 %psum.103 = f32[]{:T(128)} all-reduce(f32[]{:T(128)S(6)} %div.38), channel_id=1, replica_groups=mesh['dp'=32,'param'=16] {'dp'}, use_global_device_ids=true, to_apply=%region_18.0 | all-reduce | flops 1 | bytes 8 | tf_op jit(solution)/shard_map/psum | solution.py:74
  (1 shorter events, 0.0 us)
Async XLA Ops:
  7.2 1.0 copy-start
  7.2 4.5 copy-start.3
  7.2 5.5 copy-start.7
  7.2 119.3 %copy-start.5 = (f32[1024,36]{0,1:T(8,128)S(1)}, f32[1024,36]{0,1:T(8,128)}, u32[]{:S(2)}) copy-start(f32[1024,36]{0,1:T(8,128)} %param.10) | copy-start | bytes 442372
  7.2 119.3 %copy-start.4 = (f32[1024,36]{0,1:T(8,128)S(1)}, f32[1024,36]{0,1:T(8,128)}, u32[]{:S(2)}) copy-start(f32[1024,36]{0,1:T(8,128)} %param.11) | copy-start | bytes 442372
  7.2 119.3 %copy-start.6 = (f32[1024]{0:T(1024)S(1)}, f32[1024]{0:T(1024)}, u32[]{:S(2)}) copy-start(f32[1024]{0:T(1024)} %param.12) | copy-start | bytes 12292
  7.2 119.3 %all-reduce.9.cloned.1.call-start = ((), (), s32[]{:S(2)}) async-start(), calls=%async_computation | async-start | bytes 327680 | tf_op jit(solution)/shard_map/psum | solution.py:27
  12.6 275.0 %all-reduce.11.cloned.1.call-start = ((), (), s32[]{:S(2)}) async-start(), calls=%async_computation.1 | async-start | bytes 2097152 | tf_op jit(solution)/shard_map/psum | solution.py:40
  132.1 270.3 %all-reduce.13.cloned.1.call-start = ((), (), s32[]{:S(2)}) async-start(), calls=%async_computation.2 | async-start | bytes 327680 | tf_op jit(solution)/shard_map/psum | solution.py:27
  292.3 271.1 %copy-start.1 = (f32[2048,128]{0,1:T(8,128)S(1)}, f32[2048,128]{0,1:T(8,128)}, u32[]{:S(2)}) copy-start(f32[2048,128]{0,1:T(8,128)} %all-reduce.11.cloned.1.call-done) | copy-start | bytes 3145732
  292.3 271.1 %all-reduce.15.cloned.1.call-start = ((), (), s32[]{:S(2)}) async-start(), calls=%async_computation.3 | async-start | bytes 2097152 | tf_op jit(solution)/shard_map/psum | solution.py:40
  407.9 325.1 %all-reduce.17.cloned.1.call-start = ((), (), s32[]{:S(2)}) async-start(), calls=%async_computation.4 | async-start | bytes 327680 | tf_op jit(solution)/shard_map/psum | solution.py:27
  563.4 59.9 %copy-start.2 = (f32[2048,128]{0,1:T(8,128)S(1)}, f32[2048,128]{0,1:T(8,128)}, u32[]{:S(2)}) copy-start(f32[2048,128]{0,1:T(8,128)} %all-reduce.15.cloned.1.call-done) | copy-start | bytes 3145732
  627.7 266.3 %all-reduce.19.cloned.1.call-start = ((), (), s32[]{:S(2)}) async-start(), calls=%async_computation.5 | async-start | bytes 2097152 | tf_op jit(solution)/shard_map/psum | solution.py:40
  738.5 325.9 %all-reduce.21.cloned.1.call-start = ((), (), s32[]{:S(2)}) async-start(), calls=%async_computation.6 | async-start | bytes 327680 | tf_op jit(solution)/shard_map/psum | solution.py:27
Sparse Core Ops, SparseCore 0:
  12.7 113.7 all-reduce.8
  132.2 155.3 all-reduce.10
  292.4 109.9 all-reduce.12
  408.0 155.2 all-reduce.14
  627.8 105.1 all-reduce.16
  738.6 155.2 all-reduce.18
  959.2 105.2 all-reduce.20
where the time goes:
time: 1150 us; the launch traced here: 1140 us
  waiting for transfers between devices  899 us (78%)
  blocking collectives  168 us (15%)
  matrix products  34.5 us (3%)
  between operations  22.2 us (2%)
  other arithmetic  12.4 us (1%)
    psum x3, waiting for transfers between devices, rowsum(): return lax.psum(term, 'dp')  466 us
    psum x4, waiting for transfers between devices, head_total(): lax.psum(jnp.dot(part, w_head, preferred_element_type=jnp.float32), 'param')  433 us
    psum x4, blocking collectives, total(): return lax.psum((values[0],), 'param')  106 us
    psum x1, blocking collectives, shards(): kl_value = lax.psum(jnp.sum(dmean * dmean * inv_var) / (2.0 * batch), 'dp')  61.9 us
  transfers between devices with their start and end apart: 7, of which 7 were waited for; matrix products, arithmetic and copies ran while one was open for 0% of the time, Pallas kernels for 0%

commit v1 on v0

--- a/solution.py
+++ b/solution.py
@@ -1,6 +1,10 @@
+import functools
+
 import jax
 import jax.numpy as jnp
 from jax import lax
+from jax.experimental import pallas as pl
+from jax.experimental.pallas import tpu as pltpu
 from jax.sharding import PartitionSpec as P
 
 D = 2048
@@ -10,6 +14,150 @@
 
 DAMPING = 0.01
 TRIAL_KL = 4.0
+
+MESH = pl.DeviceIdType.MESH
+AXES = ("dp", "param")
+
+
+def _device(axis, partner):
+    return tuple(partner if name == axis else lax.axis_index(name) for name in AXES)
+
+
+def _partners(axis, n):
+    me = lax.axis_index(axis)
+    out = []
+    step = 1
+    while step < n:
+        bit = lax.rem(me // step, 2)
+        out.append((me + step - 2 * step * bit, bit))
+        step *= 2
+    return out
+
+
+def _greet(axis, partners):
+    barrier = pltpu.get_barrier_semaphore()
+    for partner, _ in partners:
+        pl.semaphore_signal(barrier, inc=1, device_id=_device(axis, partner), device_id_type=MESH)
+    pl.semaphore_wait(barrier, len(partners))
+
+
+def _halving_kernel(axis, n, x_ref, o_ref, recv, work, gat, send_a, recv_a, send_b, recv_b):
+    rows = x_ref.shape[0]
+    partners = _partners(axis, n)
+    k = len(partners)
+    _greet(axis, partners)
+    cur = x_ref
+    off = 0
+    offs = []
+    for r, (partner, bit) in enumerate(partners):
+        half = rows >> (r + 1)
+        keep = off + bit * half
+        give = off + (1 - bit) * half
+        cp = pltpu.make_async_remote_copy(
+            src_ref=cur.at[pl.ds(pl.multiple_of(give, 8), half)],
+            dst_ref=recv.at[pl.ds(0, half)] if r == 0 else recv.at[pl.ds(rows - (rows >> r), half)],
+            send_sem=send_a.at[r],
+            recv_sem=recv_a.at[r],
+            device_id=_device(axis, partner),
+            device_id_type=MESH,
+        )
+        cp.start()
+        cp.wait()
+        slot = pl.ds(0, half) if r == 0 else pl.ds(rows - (rows >> r), half)
+        kept = pl.ds(pl.multiple_of(keep, 8), half)
+        work[kept] = cur[kept] + recv[slot]
+        cur = work
+        offs.append(off)
+        off = keep
+    own = rows >> k
+    gat[pl.ds(pl.multiple_of(off, 8), own)] = work[pl.ds(pl.multiple_of(off, 8), own)]
+    for r in reversed(range(k)):
+        partner, bit = partners[r]
+        size = rows >> (r + 1)
+        cp = pltpu.make_async_remote_copy(
+            src_ref=gat.at[pl.ds(pl.multiple_of(off, 8), size)],
+            dst_ref=gat.at[pl.ds(pl.multiple_of(off, 8), size)],
+            send_sem=send_b.at[r],
+            recv_sem=recv_b.at[r],
+            device_id=_device(axis, partner),
+            device_id_type=MESH,
+        )
+        cp.start()
+        cp.wait()
+        off = offs[r]
+    o_ref[...] = gat[...]
+
+
+def _butterfly_kernel(axis, n, x_ref, o_ref, recv, acc, send_sem, recv_sem):
+    partners = _partners(axis, n)
+    k = len(partners)
+    _greet(axis, partners)
+    cur = x_ref
+    for r, (partner, _) in enumerate(partners):
+        cp = pltpu.make_async_remote_copy(
+            src_ref=cur,
+            dst_ref=recv.at[r],
+            send_sem=send_sem.at[r],
+            recv_sem=recv_sem.at[r],
+            device_id=_device(axis, partner),
+            device_id_type=MESH,
+        )
+        cp.start()
+        cp.wait()
+        dst = o_ref if r == k - 1 else acc.at[r % 2]
+        dst[...] = cur[...] + recv[r]
+        cur = dst
+
+
+_IDS = {}
+
+
+def _collective_id(key):
+    if key not in _IDS:
+        _IDS[key] = len(_IDS)
+    return _IDS[key]
+
+
+def allreduce(x, axis, n):
+    rows, cols = x.shape
+    k = n.bit_length() - 1
+    vspec = pl.BlockSpec(memory_space=pltpu.VMEM)
+    if rows % (8 * n) == 0:
+        kernel = functools.partial(_halving_kernel, axis, n)
+        scratch = [
+            pltpu.VMEM((rows, cols), jnp.float32),
+            pltpu.VMEM((rows, cols), jnp.float32),
+            pltpu.VMEM((rows, cols), jnp.float32),
+            pltpu.SemaphoreType.DMA((k,)),
+            pltpu.SemaphoreType.DMA((k,)),
+            pltpu.SemaphoreType.DMA((k,)),
+            pltpu.SemaphoreType.DMA((k,)),
+        ]
+        name = "halving"
+    else:
+        kernel = functools.partial(_butterfly_kernel, axis, n)
+        scratch = [
+            pltpu.VMEM((k, rows, cols), jnp.float32),
+            pltpu.VMEM((2, rows, cols), jnp.float32),
+            pltpu.SemaphoreType.DMA((k,)),
+            pltpu.SemaphoreType.DMA((k,)),
+        ]
+        name = "butterfly"
+    cid = _collective_id((name, axis, rows, cols))
+    return pl.pallas_call(
+        kernel,
+        out_shape=jax.ShapeDtypeStruct((rows, cols), jnp.float32),
+        in_specs=[vspec],
+        out_specs=vspec,
+        scratch_shapes=scratch,
+        compiler_params=pltpu.CompilerParams(collective_id=cid, has_side_effects=True),
+        name=f"allreduce_{name}_{axis}_{rows}x{cols}",
+    )(x)
+
+
+def scalar_sum(s, axis, n):
+    tile = jnp.broadcast_to(s.astype(jnp.float32), (8, 128))
+    return allreduce(tile, axis, n)[0, 0]
 
 
 def shards(features, w_hidden, w_head, base_mean, actions, advantages, log_std):
@@ -17,6 +165,7 @@
     rows = features.shape[0]
     width = features.shape[1]
     dp_count = lax.axis_size("dp")
+    param_count = lax.axis_size("param")
     batch = rows * dp_count
     inv_var = jnp.exp(-2.0 * log_std)
     pre = jnp.dot(features, w_hidden, preferred_element_type=jnp.float32)
@@ -24,7 +173,7 @@
     slope = 1.0 - hidden * hidden
 
     def head_total(part):
-        return lax.psum(jnp.dot(part, w_head, preferred_element_type=jnp.float32), "param")
+        return allreduce(jnp.dot(part, w_head, preferred_element_type=jnp.float32), "param", param_count)
 
     mean = base_mean + head_total(hidden.astype(jnp.bfloat16))
     delta = advantages[:, None] * (actions - mean) * inv_var
@@ -37,13 +186,13 @@
         term = lax.dot_general(
             features, grads, (((0,), (0,)), ((), ())), preferred_element_type=jnp.float32
         )
-        return lax.psum(term, "dp")
+        return allreduce(term, "dp", dp_count)
 
     def expand(vector_b):
         return jnp.dot(features, vector_b, preferred_element_type=jnp.float32)
 
     def total(values):
-        return lax.psum((values[0],), "param")
+        return (scalar_sum(values[0], "param", param_count),)
 
     grad = rowsum(pull(delta))
     solution = jnp.zeros_like(grad)
@@ -54,7 +203,6 @@
         change = expand(direction.astype(jnp.bfloat16))
         dmu = head_total((change * slope).astype(jnp.bfloat16))
         image = rowsum(pull(dmu * inv_var)) + DAMPING * direction
-        image, dmu = (image, dmu)
         (curv,) = total((jnp.sum(direction * image),))
         alpha = norm_now / curv
         solution = solution + alpha * direction
@@ -71,11 +219,12 @@
     moved = expand((reach * solution).astype(jnp.bfloat16))
     shift = (jnp.tanh(pre + moved) - hidden).astype(jnp.bfloat16)
     dmean = head_total(shift)
-    kl_value = lax.psum(jnp.sum(dmean * dmean * inv_var) / (2.0 * batch), "dp")
+    kl_value = scalar_sum(jnp.sum(dmean * dmean * inv_var) / (2.0 * batch), "dp", dp_count)
     return (step_unit, kl_value / TRIAL_KL)
 
 
 def solution(mesh):
+    _IDS.clear()
     return jax.shard_map(
         shards,
         mesh=mesh,

time: 1150 us -> 561 us (0.49)
  waiting for transfers between devices: 899 us -> 0 us
  Pallas kernels: 0 us -> 480 us
  blocking collectives: 168 us -> 0 us
  local copies, waits for them, and re-layouts: 1.67 us -> 16.7 us
  between operations: 22.2 us -> 8.63 us
    psum x7 -> x0, waiting for transfers between devices: 899 us -> none  [the longest x3 466 us: rowsum(): return lax.psum(term, 'dp')]
    pallas_call x0 -> x14, Pallas kernels: none -> 480 us  [allreduce(): pl.pallas_call(kernel, out_shape=jax.ShapeDtypeStruct((rows, cols), jnp.f...]
    psum x5 -> x0, blocking collectives: 168 us -> none  [the longest x4 106 us: total(): return lax.psum((values[0],), 'param')]
  transfers between devices with their start and end apart: 7 -> 0, of which waited for: 7 -> 0; matrix products, arithmetic and copies ran while one was open for 0% -> 0% of each run, Pallas kernels for 0% -> 0%
where the time goes in v1:
time: 561 us; the launch traced here: 557 us
  Pallas kernels  480 us (86%)
  matrix products  37.9 us (7%)
  local copies, waits for them, and re-layouts  16.7 us (3%)
  other arithmetic  13.4 us (2%)
  between operations  8.63 us (2%)
    pallas_call x14, Pallas kernels, allreduce(): pl.pallas_call(kernel, out_shape=jax.ShapeDtypeStruct((rows, cols), jnp.f...  480 us
    dot_general x3, matrix products, rowsum(): lax.dot_general(features, grads, (((0,), (0,)), ((), ())), preferred_elem...  15 us
    dot_general x4, matrix products, head_total(): jnp.dot(part, w_head, preferred_element_type=jnp.float32)  14.9 us

profile of v1, /device:TPU:1, one launch (start us, length us, event | category | flops | bytes accessed | tf_op | source)
XLA Modules:
  0.0 557.0 jit_solution(2342695263463299366)
XLA Ops:
  0.6 0.0 copy-start
  0.6 0.0 copy-start.3
  0.7 0.0 copy-start.7
  0.7 0.0 copy-start.4
  0.7 0.0 copy-start.5
  0.7 1.0 copy-done
  1.7 0.0 copy-start.6
  1.7 3.4 fusion.37
  5.1 0.0 copy-done.3
  5.1 1.0 fusion.30.x_ref
  6.1 41.0 %allreduce_halving_param_1024x36.4 = f32[1024,36]{1,0:T(8,128)} custom-call(f32[1024,36]{1,0:T(8,128)} %fusion.30.x_ref), custom_call_target="tpu_custom_call" | custom-call | tf_op jit(solution)/shard_map/allreduce_halving_param_1024x36/pallas_call | solution.py:147
  47.2 0.0 copy-done.7
  47.2 0.0 copy-done.4
  47.2 0.2 copy.15
  47.4 0.0 copy-done.5
  47.4 0.2 copy.16
  47.6 0.0 copy-done.6
  47.7 1.6 fusion.11
  49.2 4.9 convolution_bitcast_fusion.2.x_ref
  54.2 67.7 %allreduce_halving_dp_2048x128.3 = f32[2048,128]{1,0:T(8,128)} custom-call(f32[2048,128]{1,0:T(8,128)} %convolution_bitcast_fusion.2.x_ref), custom_call_target="tpu_custom_call" | custom-call | tf_op jit(solution)/shard_map/allreduce_halving_dp_2048x128/pallas_call | solution.py:147
  121.9 4.7 fusion.15.x_ref
  126.6 42.7 %allreduce_halving_param_1024x36.5 = f32[1024,36]{1,0:T(8,128)} custom-call(f32[1024,36]{1,0:T(8,128)} %fusion.15.x_ref), custom_call_target="tpu_custom_call" | custom-call | tf_op jit(solution)/shard_map/allreduce_halving_param_1024x36/pallas_call | solution.py:147
  169.3 0.0 copy-start.1
  169.3 1.5 fusion.10
  170.8 4.9 convolution_bitcast_fusion.1.x_ref
  175.7 62.2 %allreduce_halving_dp_2048x128.4 = f32[2048,128]{1,0:T(8,128)} custom-call(f32[2048,128]{1,0:T(8,128)} %convolution_bitcast_fusion.1.x_ref), custom_call_target="tpu_custom_call" | custom-call | tf_op jit(solution)/shard_map/allreduce_halving_dp_2048x128/pallas_call | solution.py:147
  238.0 0.0 copy-done.1
  238.0 0.0 copy-start.2
  238.0 2.3 multiply_reduce_fusion.4
  240.3 1.3 broadcast_in_dim.26.x_ref
  241.6 23.0 %allreduce_butterfly_param_8x128.6 = f32[8,128]{1,0:T(8,128)} custom-call(f32[8,128]{1,0:T(8,128)} %broadcast_in_dim.26.x_ref), custom_call_target="tpu_custom_call" | custom-call | tf_op jit(solution)/shard_map/allreduce_butterfly_param_8x128/pallas_call | solution.py:147
  264.6 1.2 slice.18
  265.8 1.2 broadcast_in_dim.27.x_ref
  267.0 14.9 %allreduce_butterfly_param_8x128.7 = f32[8,128]{1,0:T(8,128)} custom-call(f32[8,128]{1,0:T(8,128)} %broadcast_in_dim.27.x_ref), custom_call_target="tpu_custom_call" | custom-call | tf_op jit(solution)/shard_map/allreduce_butterfly_param_8x128/pallas_call | solution.py:147
  281.9 1.2 slice.19
  284.4 2.2 multiply_reduce_fusion.3
  286.6 1.3 broadcast_in_dim.28.x_ref
  287.9 17.1 %allreduce_butterfly_param_8x128.8 = f32[8,128]{1,0:T(8,128)} custom-call(f32[8,128]{1,0:T(8,128)} %broadcast_in_dim.28.x_ref), custom_call_target="tpu_custom_call" | custom-call | tf_op jit(solution)/shard_map/allreduce_butterfly_param_8x128/pallas_call | solution.py:147
  305.0 1.2 slice.20
  307.5 0.0 copy-done.2
  307.5 4.5 fusion.14.x_ref
  311.9 37.7 %allreduce_halving_param_1024x36.6 = f32[1024,36]{1,0:T(8,128)} custom-call(f32[1024,36]{1,0:T(8,128)} %fusion.14.x_ref), custom_call_target="tpu_custom_call" | custom-call | tf_op jit(solution)/shard_map/allreduce_halving_param_1024x36/pallas_call | solution.py:147
  349.6 1.4 fusion.9
  351.1 5.2 convolution_bitcast_fusion.x_ref
  356.2 62.6 %allreduce_halving_dp_2048x128.5 = f32[2048,128]{1,0:T(8,128)} custom-call(f32[2048,128]{1,0:T(8,128)} %convolution_bitcast_fusion.x_ref), custom_call_target="tpu_custom_call" | custom-call | tf_op jit(solution)/shard_map/allreduce_halving_dp_2048x128/pallas_call | solution.py:147
  418.9 2.3 multiply_reduce_fusion.2
  421.1 1.3 broadcast_in_dim.29.x_ref
  422.4 21.5 %allreduce_butterfly_param_8x128.9 = f32[8,128]{1,0:T(8,128)} custom-call(f32[8,128]{1,0:T(8,128)} %broadcast_in_dim.29.x_ref), custom_call_target="tpu_custom_call" | custom-call | tf_op jit(solution)/shard_map/allreduce_butterfly_param_8x128/pallas_call | solution.py:147
  443.9 1.2 slice.21
  446.4 3.5 multiply_reduce_fusion.1
  449.9 1.3 broadcast_in_dim.30.x_ref
  451.2 15.9 %allreduce_butterfly_param_8x128.10 = f32[8,128]{1,0:T(8,128)} custom-call(f32[8,128]{1,0:T(8,128)} %broadcast_in_dim.30.x_ref), custom_call_target="tpu_custom_call" | custom-call | tf_op jit(solution)/shard_map/allreduce_butterfly_param_8x128/pallas_call | solution.py:147
  467.1 1.2 broadcast_in_dim.31.x_ref
  468.3 16.1 %allreduce_butterfly_param_8x128.11 = f32[8,128]{1,0:T(8,128)} custom-call(f32[8,128]{1,0:T(8,128)} %broadcast_in_dim.31.x_ref), custom_call_target="tpu_custom_call" | custom-call | tf_op jit(solution)/shard_map/allreduce_butterfly_param_8x128/pallas_call | solution.py:147
  484.4 1.2 slice.22
  486.3 4.8 fusion.16.x_ref
  491.1 37.8 %allreduce_halving_param_1024x36.7 = f32[1024,36]{1,0:T(8,128)} custom-call(f32[1024,36]{1,0:T(8,128)} %fusion.16.x_ref), custom_call_target="tpu_custom_call" | custom-call | tf_op jit(solution)/shard_map/allreduce_halving_param_1024x36/pallas_call | solution.py:147
  528.9 1.8 multiply_reduce_fusion.6
  531.4 0.6 broadcast_in_dim.32.x_ref
  532.0 20.0 %allreduce_butterfly_dp_8x128.1 = f32[8,128]{1,0:T(8,128)} custom-call(f32[8,128]{1,0:T(8,128)} %broadcast_in_dim.32.x_ref), custom_call_target="tpu_custom_call" | custom-call | tf_op jit(solution)/shard_map/allreduce_butterfly_dp_8x128/pallas_call | solution.py:147
  552.0 1.2 slice.23
  554.5 1.4 dynamic-slice_multiply_fusion
  (1 shorter events, 0.0 us)
Async XLA Ops:
  0.6 1.0 copy-start
  0.6 4.5 copy-start.3
  0.7 46.5 %copy-start.7 = (f32[36]{0:T(128)S(1)}, f32[36]{0:T(128)}, u32[]{:S(2)}) copy-start(f32[36]{0:T(128)} %param.13) | copy-start | bytes 436
  0.7 46.5 %copy-start.4 = (f32[1024,36]{0,1:T(8,128)S(1)}, f32[1024,36]{0,1:T(8,128)}, u32[]{:S(2)}) copy-start(f32[1024,36]{0,1:T(8,128)} %param.10) | copy-start | bytes 442372
  0.7 46.7 %copy-start.5 = (f32[1024,36]{0,1:T(8,128)S(1)}, f32[1024,36]{0,1:T(8,128)}, u32[]{:S(2)}) copy-start(f32[1024,36]{0,1:T(8,128)} %param.11) | copy-start | bytes 442372
  1.7 46.0 %copy-start.6 = (f32[1024]{0:T(1024)S(1)}, f32[1024]{0:T(1024)}, u32[]{:S(2)}) copy-start(f32[1024]{0:T(1024)} %param.12) | copy-start | bytes 12292
  169.3 68.7 %copy-start.1 = (f32[2048,128]{1,0:T(8,128)S(1)}, f32[2048,128]{1,0:T(8,128)}, u32[]{:S(2)}) copy-start(f32[2048,128]{1,0:T(8,128)} %allreduce_halving_dp_2048x128.3) | copy-start | bytes 3145732
  238.0 69.5 %copy-start.2 = (f32[2048,128]{1,0:T(8,128)S(1)}, f32[2048,128]{1,0:T(8,128)}, u32[]{:S(2)}) copy-start(f32[2048,128]{1,0:T(8,128)} %allreduce_halving_dp_2048x128.4) | copy-start | bytes 3145732

commit v2 on v1

--- a/solution.py
+++ b/solution.py
@@ -109,6 +109,74 @@
         cur = dst
 
 
+def _direct_kernel(axis, n, x_ref, o_ref, recv, gat, send_a, recv_a, send_b, recv_b):
+    rows = x_ref.shape[0]
+    c = rows // n
+    me = lax.axis_index(axis)
+    peers = [(j, lax.rem(me + j, n)) for j in range(1, n)]
+    _greet(axis, [(p, None) for _, p in peers])
+    sends = []
+    for j, p in peers:
+        cp = pltpu.make_async_remote_copy(
+            src_ref=x_ref.at[pl.ds(pl.multiple_of(p * c, 8), c)],
+            dst_ref=recv.at[me],
+            send_sem=send_a.at[j],
+            recv_sem=recv_a.at[j],
+            device_id=_device(axis, p),
+            device_id_type=MESH,
+        )
+        cp.start()
+        sends.append(cp)
+    for cp in sends:
+        cp.wait()
+    mine = pl.ds(pl.multiple_of(me * c, 8), c)
+    recv[me] = x_ref[mine]
+    acc = recv[0]
+    for s in range(1, n):
+        acc = acc + recv[s]
+    gat[mine] = acc
+    sends = []
+    for j, p in peers:
+        cp = pltpu.make_async_remote_copy(
+            src_ref=gat.at[mine],
+            dst_ref=gat.at[mine],
+            send_sem=send_b.at[j],
+            recv_sem=recv_b.at[j],
+            device_id=_device(axis, p),
+            device_id_type=MESH,
+        )
+        cp.start()
+        sends.append(cp)
+    for cp in sends:
+        cp.wait()
+    o_ref[...] = gat[...]
+
+
+def _gather_sum_kernel(axis, n, x_ref, o_ref, recv, send_a, recv_a):
+    me = lax.axis_index(axis)
+    peers = [(j, lax.rem(me + j, n)) for j in range(1, n)]
+    _greet(axis, [(p, None) for _, p in peers])
+    sends = []
+    for j, p in peers:
+        cp = pltpu.make_async_remote_copy(
+            src_ref=x_ref,
+            dst_ref=recv.at[me],
+            send_sem=send_a.at[j],
+            recv_sem=recv_a.at[j],
+            device_id=_device(axis, p),
+            device_id_type=MESH,
+        )
+        cp.start()
+        sends.append(cp)
+    for cp in sends:
+        cp.wait()
+    recv[me] = x_ref[...]
+    acc = recv[0]
+    for s in range(1, n):
+        acc = acc + recv[s]
+    o_ref[...] = acc
+
+
 _IDS = {}
 
 
@@ -118,11 +186,23 @@
     return _IDS[key]
 
 
-def allreduce(x, axis, n):
+def allreduce(x, axis, n, mode="direct"):
     rows, cols = x.shape
     k = n.bit_length() - 1
     vspec = pl.BlockSpec(memory_space=pltpu.VMEM)
-    if rows % (8 * n) == 0:
+    if rows % (8 * n) != 0:
+        mode = "gather"
+    if mode == "direct":
+        kernel = functools.partial(_direct_kernel, axis, n)
+        scratch = [
+            pltpu.VMEM((n, rows // n, cols), jnp.float32),
+            pltpu.VMEM((rows, cols), jnp.float32),
+            pltpu.SemaphoreType.DMA((n,)),
+            pltpu.SemaphoreType.DMA((n,)),
+            pltpu.SemaphoreType.DMA((n,)),
+            pltpu.SemaphoreType.DMA((n,)),
+        ]
+    elif mode == "halving":
         kernel = functools.partial(_halving_kernel, axis, n)
         scratch = [
             pltpu.VMEM((rows, cols), jnp.float32),
@@ -133,17 +213,14 @@
             pltpu.SemaphoreType.DMA((k,)),
             pltpu.SemaphoreType.DMA((k,)),
         ]
-        name = "halving"
     else:
-        kernel = functools.partial(_butterfly_kernel, axis, n)
+        kernel = functools.partial(_gather_sum_kernel, axis, n)
         scratch = [
-            pltpu.VMEM((k, rows, cols), jnp.float32),
-            pltpu.VMEM((2, rows, cols), jnp.float32),
-            pltpu.SemaphoreType.DMA((k,)),
-            pltpu.SemaphoreType.DMA((k,)),
+            pltpu.VMEM((n, rows, cols), jnp.float32),
+            pltpu.SemaphoreType.DMA((n,)),
+            pltpu.SemaphoreType.DMA((n,)),
         ]
-        name = "butterfly"
-    cid = _collective_id((name, axis, rows, cols))
+    cid = _collective_id((mode, axis, rows, cols))
     return pl.pallas_call(
         kernel,
         out_shape=jax.ShapeDtypeStruct((rows, cols), jnp.float32),
@@ -151,7 +228,7 @@
         out_specs=vspec,
         scratch_shapes=scratch,
         compiler_params=pltpu.CompilerParams(collective_id=cid, has_side_effects=True),
-        name=f"allreduce_{name}_{axis}_{rows}x{cols}",
+        name=f"allreduce_{mode}_{axis}_{rows}x{cols}",
     )(x)
 
 
@@ -207,9 +284,10 @@
         alpha = norm_now / curv
         solution = solution + alpha * direction
         resid = resid - alpha * image
-        (norm_next,) = total((jnp.sum(resid * resid),))
-        direction = resid + norm_next / norm_now * direction
-        norm_now = norm_next
+        if turn + 1 < ITERS:
+            (norm_next,) = total((jnp.sum(resid * resid),))
+            direction = resid + norm_next / norm_now * direction
+            norm_now = norm_next
     (shs,) = total((jnp.sum(solution * (grad - resid)),))
     block = width // dp_count
     step_unit = lax.dynamic_slice_in_dim(

time: 561 us -> 480 us (0.86)
  Pallas kernels: 480 us -> 401 us
    pallas_call x14 -> x13, Pallas kernels: 480 us -> 401 us  [allreduce(): pl.pallas_call(kernel, out_shape=jax.ShapeDtypeStruct((rows, cols), jnp.f...]
where the time goes in v2:
time: 480 us; the launch traced here: 476 us
  Pallas kernels  401 us (84%)
  matrix products  37.9 us (8%)
  local copies, waits for them, and re-layouts  15.6 us (3%)
  other arithmetic  13.3 us (3%)
  between operations  8.62 us (2%)
    pallas_call x13, Pallas kernels, allreduce(): pl.pallas_call(kernel, out_shape=jax.ShapeDtypeStruct((rows, cols), jnp.f...  401 us
    dot_general x4, matrix products, head_total(): jnp.dot(part, w_head, preferred_element_type=jnp.float32)  15.1 us
    dot_general x3, matrix products, rowsum(): lax.dot_general(features, grads, (((0,), (0,)), ((), ())), preferred_elem...  14.8 us

profile of v2, /device:TPU:1, one launch (start us, length us, event | category | flops | bytes accessed | tf_op | source)
XLA Modules:
  0.0 476.3 jit_solution(12725339683519710662)
XLA Ops:
  0.6 0.0 copy-start
  0.6 0.0 copy-start.3
  0.7 0.0 copy-start.7
  0.7 0.0 copy-start.4
  0.7 0.0 copy-start.5
  0.7 1.0 copy-done
  1.7 0.0 copy-start.6
  1.7 3.4 fusion.42
  5.1 0.0 copy-done.3
  5.1 1.0 fusion.33.x_ref
  6.1 37.6 %allreduce_direct_param_1024x36.4 = f32[1024,36]{1,0:T(8,128)} custom-call(f32[1024,36]{1,0:T(8,128)} %fusion.33.x_ref), custom_call_target="tpu_custom_call" | custom-call | tf_op jit(solution)/shard_map/allreduce_direct_param_1024x36/pallas_call | solution.py:224
  43.7 0.0 copy-done.7
  43.8 0.0 copy-done.4
  43.8 0.2 copy.15
  44.0 0.0 copy-done.5
  44.0 0.2 copy.16
  44.2 0.0 copy-done.6
  44.2 1.6 fusion.11
  45.8 4.9 %convolution_bitcast_fusion.2.x_ref = f32[2048,128]{1,0:T(8,128)} fusion(bf16[1024,128]{1,0:T(8,128)(2,1)S(1)} %fusion.11, bf16[1024,2048]{1,0:T(8,128)(2,1)} %param.7), kind=kOutput, calls=%fused_computation.2 | convolution fusion | flops 536870912 | bytes 5505024 | tf_op jit(solution)/shard_map/dot_general | solution.py:263
  50.7 60.7 %allreduce_direct_dp_2048x128.3 = f32[2048,128]{1,0:T(8,128)} custom-call(f32[2048,128]{1,0:T(8,128)} %convolution_bitcast_fusion.2.x_ref), custom_call_target="tpu_custom_call" | custom-call | tf_op jit(solution)/shard_map/allreduce_direct_dp_2048x128/pallas_call | solution.py:224
  111.4 4.7 fusion.15.x_ref
  116.1 38.7 %allreduce_direct_param_1024x36.5 = f32[1024,36]{1,0:T(8,128)} custom-call(f32[1024,36]{1,0:T(8,128)} %fusion.15.x_ref), custom_call_target="tpu_custom_call" | custom-call | tf_op jit(solution)/shard_map/allreduce_direct_param_1024x36/pallas_call | solution.py:224
  154.8 0.0 copy-start.1
  154.8 1.5 fusion.10
  156.4 4.9 %convolution_bitcast_fusion.1.x_ref = f32[2048,128]{1,0:T(8,128)} fusion(bf16[1024,128]{1,0:T(8,128)(2,1)S(1)} %fusion.10, bf16[1024,2048]{1,0:T(8,128)(2,1)} %param.7), kind=kOutput, calls=%fused_computation.1 | convolution fusion | flops 536870912 | bytes 5505024 | tf_op jit(solution)/shard_map/dot_general | solution.py:263
  161.3 60.1 %allreduce_direct_dp_2048x128.4 = f32[2048,128]{1,0:T(8,128)} custom-call(f32[2048,128]{1,0:T(8,128)} %convolution_bitcast_fusion.1.x_ref), custom_call_target="tpu_custom_call" | custom-call | tf_op jit(solution)/shard_map/allreduce_direct_dp_2048x128/pallas_call | solution.py:224
  221.4 0.0 copy-done.1
  221.4 0.0 copy-start.2
  221.4 2.3 multiply_reduce_fusion.3
  223.7 1.3 broadcast_in_dim.23.x_ref
  225.0 14.0 %allreduce_gather_param_8x128.5 = f32[8,128]{1,0:T(8,128)} custom-call(f32[8,128]{1,0:T(8,128)} %broadcast_in_dim.23.x_ref), custom_call_target="tpu_custom_call" | custom-call | tf_op jit(solution)/shard_map/allreduce_gather_param_8x128/pallas_call | solution.py:224
  238.9 1.2 slice.18
  240.2 1.2 broadcast_in_dim.24.x_ref
  241.4 10.6 %allreduce_gather_param_8x128.6 = f32[8,128]{1,0:T(8,128)} custom-call(f32[8,128]{1,0:T(8,128)} %broadcast_in_dim.24.x_ref), custom_call_target="tpu_custom_call" | custom-call | tf_op jit(solution)/shard_map/allreduce_gather_param_8x128/pallas_call | solution.py:224
  252.0 1.2 slice.19
  254.5 2.2 multiply_reduce_fusion.2
  256.7 1.3 broadcast_in_dim.25.x_ref
  257.9 10.6 %allreduce_gather_param_8x128.7 = f32[8,128]{1,0:T(8,128)} custom-call(f32[8,128]{1,0:T(8,128)} %broadcast_in_dim.25.x_ref), custom_call_target="tpu_custom_call" | custom-call | tf_op jit(solution)/shard_map/allreduce_gather_param_8x128/pallas_call | solution.py:224
  268.5 1.2 slice.20
  271.0 0.0 copy-done.2
  271.0 4.6 fusion.14.x_ref
  275.6 33.9 %allreduce_direct_param_1024x36.6 = f32[1024,36]{1,0:T(8,128)} custom-call(f32[1024,36]{1,0:T(8,128)} %fusion.14.x_ref), custom_call_target="tpu_custom_call" | custom-call | tf_op jit(solution)/shard_map/allreduce_direct_param_1024x36/pallas_call | solution.py:224
  309.5 1.4 fusion.9
  311.0 5.0 %convolution_bitcast_fusion.x_ref = f32[2048,128]{1,0:T(8,128)} fusion(bf16[1024,128]{1,0:T(8,128)(2,1)S(1)} %fusion.9, bf16[1024,2048]{1,0:T(8,128)(2,1)} %param.7), kind=kOutput, calls=%fused_computation | convolution fusion | flops 536870912 | bytes 5505024 | tf_op jit(solution)/shard_map/dot_general | solution.py:263
  315.9 60.7 %allreduce_direct_dp_2048x128.5 = f32[2048,128]{1,0:T(8,128)} custom-call(f32[2048,128]{1,0:T(8,128)} %convolution_bitcast_fusion.x_ref), custom_call_target="tpu_custom_call" | custom-call | tf_op jit(solution)/shard_map/allreduce_direct_dp_2048x128/pallas_call | solution.py:224
  376.6 2.3 multiply_reduce_fusion.1
  378.9 1.3 broadcast_in_dim.26.x_ref
  380.2 13.5 %allreduce_gather_param_8x128.8 = f32[8,128]{1,0:T(8,128)} custom-call(f32[8,128]{1,0:T(8,128)} %broadcast_in_dim.26.x_ref), custom_call_target="tpu_custom_call" | custom-call | tf_op jit(solution)/shard_map/allreduce_gather_param_8x128/pallas_call | solution.py:224
  393.6 1.2 slice.21
  396.1 3.4 multiply_reduce_fusion
  399.6 1.3 broadcast_in_dim.27.x_ref
  400.9 10.6 %allreduce_gather_param_8x128.9 = f32[8,128]{1,0:T(8,128)} custom-call(f32[8,128]{1,0:T(8,128)} %broadcast_in_dim.27.x_ref), custom_call_target="tpu_custom_call" | custom-call | tf_op jit(solution)/shard_map/allreduce_gather_param_8x128/pallas_call | solution.py:224
  411.4 1.2 slice.22
  413.3 4.8 %fusion.16.x_ref = f32[1024,36]{1,0:T(8,128)} fusion(bf16[128,36]{0,1:T(8,128)(2,1)S(1)} %copy-done.3, f32[1024,128]{1,0:T(8,128)S(1)} %fusion.42, bf16[1024,2048]{1,0:T(8,128)(2,1)} %param.7, f32[2048,128]{1,0:T(8,128)} %get-tuple-element.5, f32[]{:T(128)} %bitcast.9), kind=kOutput, calls=%fused_computation.25 | convolution fusion | flops 547225600 | bytes 5923844 | tf_op jit(solution)/shard_map/dot_general | solution.py:253
  418.1 33.5 %allreduce_direct_param_1024x36.7 = f32[1024,36]{1,0:T(8,128)} custom-call(f32[1024,36]{1,0:T(8,128)} %fusion.16.x_ref), custom_call_target="tpu_custom_call" | custom-call | tf_op jit(solution)/shard_map/allreduce_direct_param_1024x36/pallas_call | solution.py:224
  451.7 1.8 multiply_reduce_fusion.5
  454.1 0.6 broadcast_in_dim.28.x_ref
  454.7 16.5 %allreduce_gather_dp_8x128.1 = f32[8,128]{1,0:T(8,128)} custom-call(f32[8,128]{1,0:T(8,128)} %broadcast_in_dim.28.x_ref), custom_call_target="tpu_custom_call" | custom-call | tf_op jit(solution)/shard_map/allreduce_gather_dp_8x128/pallas_call | solution.py:224
  471.2 1.2 slice.23
  473.8 1.4 dynamic-slice_multiply_fusion
  (1 shorter events, 0.0 us)
Async XLA Ops:
  0.6 1.0 copy-start
  0.6 4.5 copy-start.3
  0.7 43.1 %copy-start.7 = (f32[36]{0:T(128)S(1)}, f32[36]{0:T(128)}, u32[]{:S(2)}) copy-start(f32[36]{0:T(128)} %param.13) | copy-start | bytes 436
  0.7 43.1 %copy-start.4 = (f32[1024,36]{0,1:T(8,128)S(1)}, f32[1024,36]{0,1:T(8,128)}, u32[]{:S(2)}) copy-start(f32[1024,36]{0,1:T(8,128)} %param.10) | copy-start | bytes 442372
  0.7 43.3 %copy-start.5 = (f32[1024,36]{0,1:T(8,128)S(1)}, f32[1024,36]{0,1:T(8,128)}, u32[]{:S(2)}) copy-start(f32[1024,36]{0,1:T(8,128)} %param.11) | copy-start | bytes 442372
  1.7 42.5 %copy-start.6 = (f32[1024]{0:T(1024)S(1)}, f32[1024]{0:T(1024)}, u32[]{:S(2)}) copy-start(f32[1024]{0:T(1024)} %param.12) | copy-start | bytes 12292
  154.8 66.6 %copy-start.1 = (f32[2048,128]{1,0:T(8,128)S(1)}, f32[2048,128]{1,0:T(8,128)}, u32[]{:S(2)}) copy-start(f32[2048,128]{1,0:T(8,128)} %allreduce_direct_dp_2048x128.3) | copy-start | bytes 3145732
  221.4 49.6 %copy-start.2 = (f32[2048,128]{1,0:T(8,128)S(1)}, f32[2048,128]{1,0:T(8,128)}, u32[]{:S(2)}) copy-start(f32[2048,128]{1,0:T(8,128)} %allreduce_direct_dp_2048x128.4) | copy-start | bytes 3145732

commit v3 on v2

--- a/solution.py
+++ b/solution.py
@@ -232,6 +232,162 @@
     )(x)
 
 
+def _tile_sum(x):
+    return jnp.sum(jnp.sum(x, axis=0, keepdims=True), axis=1, keepdims=True)
+
+
+def _cg_kernel(mode, n_dp, n_pa, *refs):
+    if mode == "first":
+        part_ref = refs[0]
+        ins = 1
+    elif mode == "iter":
+        part_ref, p_ref, r_ref, x_ref, rr_ref = refs[:5]
+        ins = 5
+    else:
+        part_ref, p_ref, r_ref, x_ref, rr_ref, g_ref = refs[:6]
+        ins = 6
+    nout = {"first": 3, "iter": 5, "last": 2}[mode]
+    outs = refs[ins:ins + nout]
+    recv, gat, tiles, srecv, send_a, recv_a, send_b, recv_b, send_s, recv_s = refs[ins + nout:]
+    rows = part_ref.shape[0]
+    c = rows // n_dp
+    me = lax.axis_index("dp")
+    mp = lax.axis_index("param")
+    dpeers = [(j, lax.rem(me + j, n_dp)) for j in range(1, n_dp)]
+    ppeers = [(j, lax.rem(mp + j, n_pa)) for j in range(1, n_pa)]
+    barrier = pltpu.get_barrier_semaphore()
+    for _, p in dpeers:
+        pl.semaphore_signal(barrier, inc=1, device_id=_device("dp", p), device_id_type=MESH)
+    for _, p in ppeers:
+        pl.semaphore_signal(barrier, inc=1, device_id=_device("param", p), device_id_type=MESH)
+    pl.semaphore_wait(barrier, len(dpeers) + len(ppeers))
+    sends = []
+    for j, p in dpeers:
+        cp = pltpu.make_async_remote_copy(
+            src_ref=part_ref.at[pl.ds(pl.multiple_of(p * c, 8), c)],
+            dst_ref=recv.at[me],
+            send_sem=send_a.at[j],
+            recv_sem=recv_a.at[j],
+            device_id=_device("dp", p),
+            device_id_type=MESH,
+        )
+        cp.start()
+        sends.append(cp)
+    for cp in sends:
+        cp.wait()
+    mine = pl.ds(pl.multiple_of(me * c, 8), c)
+    recv[me] = part_ref[mine]
+    acc = recv[0]
+    for s in range(1, n_dp):
+        acc = acc + recv[s]
+    gat[mine] = acc
+    sends = []
+    for j, p in dpeers:
+        cp = pltpu.make_async_remote_copy(
+            src_ref=gat.at[mine],
+            dst_ref=gat.at[mine],
+            send_sem=send_b.at[j],
+            recv_sem=recv_b.at[j],
+            device_id=_device("dp", p),
+            device_id_type=MESH,
+        )
+        cp.start()
+        sends.append(cp)
+    for cp in sends:
+        cp.wait()
+
+    def psum_param(k, value):
+        tiles[k] = jnp.broadcast_to(value, tiles.shape[1:])
+        sends = []
+        for j, p in ppeers:
+            cp = pltpu.make_async_remote_copy(
+                src_ref=tiles.at[k],
+                dst_ref=srecv.at[k, mp],
+                send_sem=send_s.at[k, j],
+                recv_sem=recv_s.at[k, j],
+                device_id=_device("param", p),
+                device_id_type=MESH,
+            )
+            cp.start()
+            sends.append(cp)
+        for cp in sends:
+            cp.wait()
+        srecv[k, mp] = tiles[k]
+        total = srecv[k, 0]
+        for s in range(1, n_pa):
+            total = total + srecv[k, s]
+        return total[0:1, 0:1]
+
+    if mode == "first":
+        grad_out, pb_out, rr_out = outs
+        grad = gat[...]
+        grad_out[...] = grad
+        pb_out[...] = grad.astype(jnp.bfloat16)
+        rr = psum_param(0, _tile_sum(grad * grad))
+        rr_out[...] = jnp.broadcast_to(rr, rr_out.shape)
+        return
+    direction = p_ref[...]
+    rr = rr_ref[0:1, 0:1]
+    image = gat[...] + DAMPING * direction
+    curv = psum_param(0, _tile_sum(direction * image))
+    alpha = rr / curv
+    x_new = x_ref[...] + alpha * direction
+    r_new = r_ref[...] - alpha * image
+    if mode == "iter":
+        x_out, r_out, p_out, pb_out, rr_out = outs
+        x_out[...] = x_new
+        r_out[...] = r_new
+        rr_next = psum_param(1, _tile_sum(r_new * r_new))
+        p_new = r_new + rr_next / rr * direction
+        p_out[...] = p_new
+        pb_out[...] = p_new.astype(jnp.bfloat16)
+        rr_out[...] = jnp.broadcast_to(rr_next, rr_out.shape)
+        return
+    step_out, moved_out = outs
+    shs = psum_param(1, _tile_sum(x_new * (g_ref[...] - r_new)))
+    gat[...] = x_new
+    blk = step_out.shape[0]
+    step_out[...] = gat[pl.ds(pl.multiple_of(me * blk, 8), blk)] * jnp.sqrt(D * UNITS / shs)
+    reach = jnp.sqrt(2.0 * TRIAL_KL / shs)
+    moved_out[...] = (reach * x_new).astype(jnp.bfloat16)
+
+
+def cg_step(mode, n_dp, n_pa, block, *args):
+    rows, cols = args[0].shape
+    f32, bf16 = jnp.float32, jnp.bfloat16
+    big = jax.ShapeDtypeStruct((rows, cols), f32)
+    tile = jax.ShapeDtypeStruct((8, 128), f32)
+    if mode == "first":
+        out_shape = (big, jax.ShapeDtypeStruct((rows, cols), bf16), tile)
+    elif mode == "iter":
+        out_shape = (big, big, big, jax.ShapeDtypeStruct((rows, cols), bf16), tile)
+    else:
+        out_shape = (jax.ShapeDtypeStruct((block, cols), f32), jax.ShapeDtypeStruct((rows, cols), bf16))
+    vspec = pl.BlockSpec(memory_space=pltpu.VMEM)
+    scratch = [
+        pltpu.VMEM((n_dp, rows // n_dp, cols), f32),
+        pltpu.VMEM((rows, cols), f32),
+        pltpu.VMEM((2, 8, 128), f32),
+        pltpu.VMEM((2, n_pa, 8, 128), f32),
+        pltpu.SemaphoreType.DMA((n_dp,)),
+        pltpu.SemaphoreType.DMA((n_dp,)),
+        pltpu.SemaphoreType.DMA((n_dp,)),
+        pltpu.SemaphoreType.DMA((n_dp,)),
+        pltpu.SemaphoreType.DMA((2, n_pa)),
+        pltpu.SemaphoreType.DMA((2, n_pa)),
+    ]
+    cid = _collective_id(("cg", mode, rows, cols))
+    return pl.pallas_call(
+        functools.partial(_cg_kernel, mode, n_dp, n_pa),
+        out_shape=out_shape,
+        in_specs=[vspec] * len(args),
+        out_specs=tuple([vspec] * len(out_shape)),
+        scratch_shapes=scratch,
+        compiler_params=pltpu.CompilerParams(collective_id=cid, has_side_effects=True),
+        name=f"cg_{mode}",
+    )(*args)
+
+
 def scalar_sum(s, axis, n):
     tile = jnp.broadcast_to(s.astype(jnp.float32), (8, 128))
     return allreduce(tile, axis, n)[0, 0]
@@ -250,7 +406,13 @@
     slope = 1.0 - hidden * hidden
 
     def head_total(part):
-        return allreduce(jnp.dot(part, w_head, preferred_element_type=jnp.float32), "param", param_count)
+        local = jnp.dot(part, w_head, preferred_element_type=jnp.float32)
+        shape = local.shape
+        flat = local.reshape(-1, 128)
+        lanes = flat.shape[0]
+        tall = -(-lanes // (8 * param_count)) * 8 * param_count
+        flat = jnp.pad(flat, ((0, tall - lanes), (0, 0)))
+        return allreduce(flat, "param", param_count)[:lanes].reshape(shape)
 
     mean = base_mean + head_total(hidden.astype(jnp.bfloat16))
     delta = advantages[:, None] * (actions - mean) * inv_var
@@ -260,41 +422,31 @@
         return (jnp.dot(moment, head_t, precision=highest) * slope / batch).astype(jnp.bfloat16)
 
     def rowsum(grads):
-        term = lax.dot_general(
+        return lax.dot_general(
             features, grads, (((0,), (0,)), ((), ())), preferred_element_type=jnp.float32
         )
-        return allreduce(term, "dp", dp_count)
 
     def expand(vector_b):
         return jnp.dot(features, vector_b, preferred_element_type=jnp.float32)
 
-    def total(values):
-        return (scalar_sum(values[0], "param", param_count),)
-
-    grad = rowsum(pull(delta))
+    block = width // dp_count
+    grad, direction_b, rr = cg_step("first", dp_count, param_count, block, rowsum(pull(delta)))
+    direction = grad
+    resid = grad
     solution = jnp.zeros_like(grad)
-    resid = grad
-    direction = grad
-    (norm_now,) = total((jnp.sum(resid * resid),))
     for turn in range(ITERS):
-        change = expand(direction.astype(jnp.bfloat16))
+        change = expand(direction_b)
         dmu = head_total((change * slope).astype(jnp.bfloat16))
-        image = rowsum(pull(dmu * inv_var)) + DAMPING * direction
-        (curv,) = total((jnp.sum(direction * image),))
-        alpha = norm_now / curv
-        solution = solution + alpha * direction
-        resid = resid - alpha * image
+        partial = rowsum(pull(dmu * inv_var))
         if turn + 1 < ITERS:
-            (norm_next,) = total((jnp.sum(resid * resid),))
-            direction = resid + norm_next / norm_now * direction
-            norm_now = norm_next
-    (shs,) = total((jnp.sum(solution * (grad - resid)),))
-    block = width // dp_count
-    step_unit = lax.dynamic_slice_in_dim(
-        solution * jnp.sqrt(D * UNITS / shs), lax.axis_index("dp") * block, block, 0
-    )
-    reach = jnp.sqrt(2.0 * TRIAL_KL / shs)
-    moved = expand((reach * solution).astype(jnp.bfloat16))
+            solution, resid, direction, direction_b, rr = cg_step(
+                "iter", dp_count, param_count, block, partial, direction, resid, solution, rr
+            )
+        else:
+            step_unit, moved_b = cg_step(
+                "last", dp_count, param_count, block, partial, direction, resid, solution, rr, grad
+            )
+    moved = expand(moved_b)
     shift = (jnp.tanh(pre + moved) - hidden).astype(jnp.bfloat16)
     dmean = head_total(shift)
     kl_value = scalar_sum(jnp.sum(dmean * dmean * inv_var) / (2.0 * batch), "dp", dp_count)

time: 480 us -> 377 us (0.79)
  Pallas kernels: 401 us -> 324 us
  other arithmetic: 13.3 us -> 1.56 us
  matrix products: 37.9 us -> 31.7 us
  between operations: 8.62 us -> 3.31 us
    pallas_call x13 -> x5, Pallas kernels: 401 us -> 103 us  [allreduce(): pl.pallas_call(kernel, out_shape=jax.ShapeDtypeStruct((rows, cols), jnp.f...]
    pallas_call x0 -> x3, Pallas kernels: none -> 221 us  [cg_step(): pl.pallas_call(functools.partial(_cg_kernel, mode, n_dp, n_pa), out_shape...]
    reduce_sum x4 -> x0, other arithmetic: 10.1 us -> none  [the longest x2 4.52 us: shards(): curv, = total((jnp.sum(direction * image),))]
    broadcast_in_dim x6 -> x1, local copies, waits for them, and re-layouts: 6.96 us -> 0.6 us  [scalar_sum(): tile = jnp.broadcast_to(s.astype(jnp.float32), (8, 128))]
    slice x6 -> x1, local copies, waits for them, and re-layouts: 7.16 us -> 1.18 us  [scalar_sum(): return allreduce(tile, axis, n)[0, 0]]
where the time goes in v3:
time: 377 us; the launch traced here: 376 us
  Pallas kernels  324 us (86%)
  matrix products  31.7 us (8%)
  local copies, waits for them, and re-layouts  14.7 us (4%)
    pallas_call x3, Pallas kernels, cg_step(): pl.pallas_call(functools.partial(_cg_kernel, mode, n_dp, n_pa), out_shape...  221 us
    pallas_call x5, Pallas kernels, allreduce(): pl.pallas_call(kernel, out_shape=jax.ShapeDtypeStruct((rows, cols), jnp.f...  103 us
    dot_general x3, matrix products, rowsum(): lax.dot_general(features, grads, (((0,), (0,)), ((), ())), preferred_elem...  14.8 us
    dot_general x4, matrix products, head_total(): local = jnp.dot(part, w_head, preferred_element_type=jnp.float32)  11.4 us

profile of v3, /device:TPU:1, one launch (start us, length us, event | category | flops | bytes accessed | tf_op | source)
XLA Modules:
  0.0 375.7 jit_solution(408667059540403348)
XLA Ops:
  0.6 0.0 copy-start
  0.6 0.0 copy-start.1
  0.7 0.0 copy-start.6
  0.7 0.0 copy-start.3
  0.7 0.0 copy-start.2
  0.7 1.0 copy-done
  1.7 0.0 copy-start.5
  1.7 3.4 fusion.31
  5.1 0.0 copy-done.1
  5.1 0.2 fusion.18
  5.4 0.4 reshape.31
  5.8 0.7 pad.13.x_ref
  6.5 25.1 %allreduce_direct_param_384x128.4 = f32[384,128]{1,0:T(8,128)} custom-call(f32[384,128]{1,0:T(8,128)} %pad.13.x_ref), custom_call_target="tpu_custom_call" | custom-call | tf_op jit(solution)/shard_map/allreduce_direct_param_384x128/pallas_call | solution.py:224
  31.6 0.9 slice.15
  32.5 0.6 reshape.32
  33.2 0.2 copy.30
  33.4 0.0 copy-done.6
  33.4 0.0 copy-done.3
  33.4 0.0 copy-done.2
  33.4 0.0 copy-done.5
  33.4 0.7 fusion.11
  34.1 5.0 %convolution_bitcast_fusion.2.refs_0_ = f32[2048,128]{1,0:T(8,128)} fusion(bf16[1024,128]{1,0:T(8,128)(2,1)S(1)} %fusion.11, bf16[1024,2048]{1,0:T(8,128)(2,1)} %param.7), kind=kOutput, calls=%fused_computation.2 | convolution fusion | flops 536870912 | bytes 5505024 | tf_op jit(solution)/shard_map/dot_general | solution.py:425
  39.1 69.7 %cg_first.1 = (f32[2048,128]{1,0:T(8,128)}, bf16[2048,128]{1,0:T(8,128)(2,1)}, f32[8,128]{1,0:T(8,128)}) custom-call(f32[2048,128]{1,0:T(8,128)} %convolution_bitcast_fusion.2.refs_0_), custom_call_target="tpu_custom_call" | custom-call | tf_op jit(solution)/shard_map/cg_first/pallas_call | solution.py:380
  108.8 3.7 fusion.15
  112.6 0.4 reshape.33
  113.0 0.7 pad.14.x_ref
  113.7 20.4 %allreduce_direct_param_384x128.5 = f32[384,128]{1,0:T(8,128)} custom-call(f32[384,128]{1,0:T(8,128)} %pad.14.x_ref), custom_call_target="tpu_custom_call" | custom-call | tf_op jit(solution)/shard_map/allreduce_direct_param_384x128/pallas_call | solution.py:224
  134.1 0.9 slice.16
  135.0 0.6 reshape.34
  135.7 0.2 copy.34
  135.9 0.7 fusion.10
  136.6 4.9 %convolution_bitcast_fusion.1.refs_0_ = f32[2048,128]{1,0:T(8,128)} fusion(bf16[1024,128]{1,0:T(8,128)(2,1)S(1)} %fusion.10, bf16[1024,2048]{1,0:T(8,128)(2,1)} %param.7), kind=kOutput, calls=%fused_computation.1 | convolution fusion | flops 536870912 | bytes 5505024 | tf_op jit(solution)/shard_map/dot_general | solution.py:425
  141.5 1.1 broadcast_in_dim.4.refs_3_
  142.6 76.3 %cg_iter.1 = (f32[2048,128]{1,0:T(8,128)}, f32[2048,128]{1,0:T(8,128)}, f32[2048,128]{1,0:T(8,128)}, bf16[2048,128]{1,0:T(8,128)(2,1)}, f32[8,128]{1,0:T(8,128)}) custom-call(f32[2048,128]{1,0:T(8,128)} %convolution_bitcast_fusion.1.refs_0_, f32[2048,128]{1,0:T(8,128)} %get-tuple-element.13.refs_1_.refs_2_.refs_5_, ...), custom_call_target="tpu_custom_call" | custom-call | tf_op jit(solution)/shard_map/cg_iter/pallas_call | solution.py:380
  218.8 3.7 fusion.14
  222.6 0.4 reshape.35
  223.0 0.7 pad.15.x_ref
  223.7 21.2 %allreduce_direct_param_384x128.6 = f32[384,128]{1,0:T(8,128)} custom-call(f32[384,128]{1,0:T(8,128)} %pad.15.x_ref), custom_call_target="tpu_custom_call" | custom-call | tf_op jit(solution)/shard_map/allreduce_direct_param_384x128/pallas_call | solution.py:224
  244.9 0.9 slice.17
  245.8 0.6 reshape.36
  246.4 0.2 copy.38
  246.6 0.7 fusion.9
  247.3 4.9 %convolution_bitcast_fusion.refs_0_ = f32[2048,128]{1,0:T(8,128)} fusion(bf16[1024,128]{1,0:T(8,128)(2,1)S(1)} %fusion.9, bf16[1024,2048]{1,0:T(8,128)(2,1)} %param.7), kind=kOutput, calls=%fused_computation | convolution fusion | flops 536870912 | bytes 5505024 | tf_op jit(solution)/shard_map/dot_general | solution.py:425
  252.2 75.1 %cg_last.1 = (f32[64,128]{1,0:T(8,128)}, bf16[2048,128]{1,0:T(8,128)(2,1)}) custom-call(f32[2048,128]{1,0:T(8,128)} %convolution_bitcast_fusion.refs_0_, f32[2048,128]{1,0:T(8,128)} %get-tuple-element.16.refs_1_, f32[2048,128]{1,0:T(8,128)} %get-tuple-element.17.refs_2_, f32[2048,128]{1,0:T(8,128)} %get-tuple-element.18.refs_3_, ...), custom_call_target="tpu_custom_call" | custom-call | tf_op jit(solution)/shard_map/cg_last/pallas_call | solution.py:380
  327.4 0.0 copy-start.4
  327.4 3.8 fusion.16
  331.1 0.4 reshape.37
  331.6 0.7 pad.16.x_ref
  332.3 21.2 %allreduce_direct_param_384x128.7 = f32[384,128]{1,0:T(8,128)} custom-call(f32[384,128]{1,0:T(8,128)} %pad.16.x_ref), custom_call_target="tpu_custom_call" | custom-call | tf_op jit(solution)/shard_map/allreduce_direct_param_384x128/pallas_call | solution.py:224
  353.5 0.4 mul.80
  354.0 1.6 multiply_reduce_fusion
  356.2 0.6 broadcast_in_dim.5.x_ref
  356.8 15.3 %allreduce_gather_dp_8x128.1 = f32[8,128]{1,0:T(8,128)} custom-call(f32[8,128]{1,0:T(8,128)} %broadcast_in_dim.5.x_ref), custom_call_target="tpu_custom_call" | custom-call | tf_op jit(solution)/shard_map/allreduce_gather_dp_8x128/pallas_call | solution.py:224
  372.1 1.2 slice.19
  373.9 0.0 copy-done.4
  373.9 0.6 copy.54
  (2 shorter events, 0.0 us)
Async XLA Ops:
  0.6 1.0 copy-start
  0.6 4.5 %copy-start.1 = (bf16[128,36]{0,1:T(8,128)(2,1)S(1)}, bf16[128,36]{0,1:T(8,128)(2,1)}, u32[]{:S(2)}) copy-start(bf16[128,36]{0,1:T(8,128)(2,1)} %param.9) | copy-start | bytes 27652
  0.7 32.7 %copy-start.6 = (f32[36]{0:T(128)S(1)}, f32[36]{0:T(128)}, u32[]{:S(2)}) copy-start(f32[36]{0:T(128)} %param.13) | copy-start | bytes 436
  0.7 32.7 %copy-start.3 = (f32[1024,36]{0,1:T(8,128)S(1)}, f32[1024,36]{0,1:T(8,128)}, u32[]{:S(2)}) copy-start(f32[1024,36]{0,1:T(8,128)} %param.10) | copy-start | bytes 442372
  0.7 32.7 %copy-start.2 = (f32[1024,36]{0,1:T(8,128)S(1)}, f32[1024,36]{0,1:T(8,128)}, u32[]{:S(2)}) copy-start(f32[1024,36]{0,1:T(8,128)} %param.11) | copy-start | bytes 442372
  1.7 31.7 %copy-start.5 = (f32[1024]{0:T(1024)S(1)}, f32[1024]{0:T(1024)}, u32[]{:S(2)}) copy-start(f32[1024]{0:T(1024)} %param.12) | copy-start | bytes 12292
  327.4 46.6 %copy-start.4 = (f32[64,128]{1,0:T(8,128)S(1)}, f32[64,128]{1,0:T(8,128)}, u32[]{:S(2)}) copy-start(f32[64,128]{1,0:T(8,128)} %get-tuple-element.24) | copy-start | bytes 98308

commit v4 on v3

--- a/solution.py
+++ b/solution.py
@@ -255,6 +255,8 @@
     mp = lax.axis_index("param")
     dpeers = [(j, lax.rem(me + j, n_dp)) for j in range(1, n_dp)]
     ppeers = [(j, lax.rem(mp + j, n_pa)) for j in range(1, n_pa)]
+    if mode == "first":
+        ppeers = []
     barrier = pltpu.get_barrier_semaphore()
     for _, p in dpeers:
         pl.semaphore_signal(barrier, inc=1, device_id=_device("dp", p), device_id_type=MESH)
@@ -296,8 +298,12 @@
     for cp in sends:
         cp.wait()
 
-    def psum_param(k, value):
-        tiles[k] = jnp.broadcast_to(value, tiles.shape[1:])
+    def psum_param(k, values):
+        row = lax.broadcasted_iota(jnp.int32, tiles.shape[1:], 0)
+        tile = jnp.zeros(tiles.shape[1:], jnp.float32)
+        for i, v in enumerate(values):
+            tile = jnp.where(row == i, jnp.broadcast_to(v, tile.shape), tile)
+        tiles[k] = tile
         sends = []
         for j, p in ppeers:
             cp = pltpu.make_async_remote_copy(
@@ -316,35 +322,44 @@
         total = srecv[k, 0]
         for s in range(1, n_pa):
             total = total + srecv[k, s]
-        return total[0:1, 0:1]
+        return [total[i:i + 1, 0:1] for i in range(len(values))]
 
     if mode == "first":
         grad_out, pb_out, rr_out = outs
         grad = gat[...]
         grad_out[...] = grad
         pb_out[...] = grad.astype(jnp.bfloat16)
-        rr = psum_param(0, _tile_sum(grad * grad))
-        rr_out[...] = jnp.broadcast_to(rr, rr_out.shape)
+        rr_out[...] = jnp.broadcast_to(_tile_sum(grad * grad), rr_out.shape)
         return
     direction = p_ref[...]
+    resid = r_ref[...]
     rr = rr_ref[0:1, 0:1]
     image = gat[...] + DAMPING * direction
-    curv = psum_param(0, _tile_sum(direction * image))
-    alpha = rr / curv
-    x_new = x_ref[...] + alpha * direction
-    r_new = r_ref[...] - alpha * image
     if mode == "iter":
+        curv, r_img, img_img = psum_param(
+            0, [_tile_sum(direction * image), _tile_sum(resid * image), _tile_sum(image * image)]
+        )
+        alpha = rr / curv
         x_out, r_out, p_out, pb_out, rr_out = outs
-        x_out[...] = x_new
+        x_out[...] = x_ref[...] + alpha * direction
+        r_new = resid - alpha * image
         r_out[...] = r_new
-        rr_next = psum_param(1, _tile_sum(r_new * r_new))
+        rr_next = rr - 2.0 * alpha * r_img + alpha * alpha * img_img
         p_new = r_new + rr_next / rr * direction
         p_out[...] = p_new
         pb_out[...] = p_new.astype(jnp.bfloat16)
         rr_out[...] = jnp.broadcast_to(rr_next, rr_out.shape)
         return
+    sol = x_ref[...]
+    gap = g_ref[...] - resid
+    curv, x_gap, x_img, p_gap = psum_param(
+        0,
+        [_tile_sum(direction * image), _tile_sum(sol * gap), _tile_sum(sol * image), _tile_sum(direction * gap)],
+    )
+    alpha = rr / curv
+    x_new = sol + alpha * direction
+    shs = x_gap + alpha * (x_img + p_gap) + alpha * alpha * curv
     step_out, moved_out = outs
-    shs = psum_param(1, _tile_sum(x_new * (g_ref[...] - r_new)))
     gat[...] = x_new
     blk = step_out.shape[0]
     step_out[...] = gat[pl.ds(pl.multiple_of(me * blk, 8), blk)] * jnp.sqrt(D * UNITS / shs)
@@ -388,6 +403,137 @@
     )(*args)
 
 
+def _head_kernel(n, n_dp, extra, kl, *refs):
+    refs = list(refs)
+    x_ref = refs.pop(0)
+    e_ref = refs.pop(0) if extra else None
+    iv_ref = refs.pop(0) if kl else None
+    o_ref = refs.pop(0)
+    eo_ref = refs.pop(0) if (extra or kl) else None
+    recv, gat, erecv, send_a, recv_a, send_b, recv_b, send_e, recv_e = refs
+    rows = x_ref.shape[0]
+    c = rows // n
+    me = lax.axis_index("param")
+    md = lax.axis_index("dp")
+    peers = [(j, lax.rem(me + j, n)) for j in range(1, n)]
+    dpeers = [(j, lax.rem(md + j, n_dp)) for j in range(1, n_dp)] if kl else []
+    barrier = pltpu.get_barrier_semaphore()
+    for _, p in peers:
+        pl.semaphore_signal(barrier, inc=1, device_id=_device("param", p), device_id_type=MESH)
+    for _, p in dpeers:
+        pl.semaphore_signal(barrier, inc=1, device_id=_device("dp", p), device_id_type=MESH)
+    pl.semaphore_wait(barrier, len(peers) + len(dpeers))
+    sends = []
+    for j, p in peers:
+        cp = pltpu.make_async_remote_copy(
+            src_ref=x_ref.at[pl.ds(pl.multiple_of(p * c, 8), c)],
+            dst_ref=recv.at[me],
+            send_sem=send_a.at[j],
+            recv_sem=recv_a.at[j],
+            device_id=_device("param", p),
+            device_id_type=MESH,
+        )
+        cp.start()
+        sends.append(cp)
+        if extra:
+            cp = pltpu.make_async_remote_copy(
+                src_ref=e_ref,
+                dst_ref=erecv.at[me],
+                send_sem=send_e.at[j],
+                recv_sem=recv_e.at[j],
+                device_id=_device("param", p),
+                device_id_type=MESH,
+            )
+            cp.start()
+            sends.append(cp)
+    for cp in sends:
+        cp.wait()
+    mine = pl.ds(pl.multiple_of(me * c, 8), c)
+    recv[me] = x_ref[mine]
+    acc = recv[0]
+    for s in range(1, n):
+        acc = acc + recv[s]
+    gat[mine] = acc
+    if extra:
+        erecv[me] = e_ref[...]
+        etot = erecv[0]
+        for s in range(1, n):
+            etot = etot + erecv[s]
+        eo_ref[...] = etot
+    sends = []
+    for j, p in peers:
+        cp = pltpu.make_async_remote_copy(
+            src_ref=gat.at[mine],
+            dst_ref=gat.at[mine],
+            send_sem=send_b.at[j],
+            recv_sem=recv_b.at[j],
+            device_id=_device("param", p),
+            device_id_type=MESH,
+        )
+        cp.start()
+        sends.append(cp)
+    for cp in sends:
+        cp.wait()
+    total = gat[...]
+    o_ref[...] = total
+    if kl:
+        local = _tile_sum(total * total * iv_ref[...])
+        erecv[0] = jnp.broadcast_to(local, erecv.shape[1:])
+        sends = []
+        for j, p in dpeers:
+            cp = pltpu.make_async_remote_copy(
+                src_ref=erecv.at[0],
+                dst_ref=erecv.at[1 + md],
+                send_sem=send_e.at[j],
+                recv_sem=recv_e.at[j],
+                device_id=_device("dp", p),
+                device_id_type=MESH,
+            )
+            cp.start()
+            sends.append(cp)
+        for cp in sends:
+            cp.wait()
+        erecv[1 + md] = erecv[0]
+        ktot = erecv[1]
+        for s in range(1, n_dp):
+            ktot = ktot + erecv[1 + s]
+        eo_ref[...] = ktot
+
+
+def head_allreduce(flat, n, n_dp, tile=None, ivflat=None):
+    rows, cols = flat.shape
+    f32 = jnp.float32
+    extra = tile is not None
+    kl = ivflat is not None
+    args = [flat] + ([tile] if extra else []) + ([ivflat] if kl else [])
+    out_shape = [jax.ShapeDtypeStruct((rows, cols), f32)]
+    if extra or kl:
+        out_shape.append(jax.ShapeDtypeStruct((8, 128), f32))
+    m = max(n, n_dp + 1) if kl else n
+    vspec = pl.BlockSpec(memory_space=pltpu.VMEM)
+    scratch = [
+        pltpu.VMEM((n, rows // n, cols), f32),
+        pltpu.VMEM((rows, cols), f32),
+        pltpu.VMEM((m, 8, 128), f32),
+        pltpu.SemaphoreType.DMA((n,)),
+        pltpu.SemaphoreType.DMA((n,)),
+        pltpu.SemaphoreType.DMA((n,)),
+        pltpu.SemaphoreType.DMA((n,)),
+        pltpu.SemaphoreType.DMA((max(n, n_dp),)),
+        pltpu.SemaphoreType.DMA((max(n, n_dp),)),
+    ]
+    cid = _collective_id(("head", extra, kl, rows, cols))
+    return pl.pallas_call(
+        functools.partial(_head_kernel, n, n_dp, extra, kl),
+        out_shape=tuple(out_shape),
+        in_specs=[vspec] * len(args),
+        out_specs=tuple([vspec] * len(out_shape)),
+        scratch_shapes=scratch,
+        compiler_params=pltpu.CompilerParams(collective_id=cid, has_side_effects=True),
+        name=f"head_allreduce_{int(extra)}{int(kl)}",
+    )(*args)
+
+
 def scalar_sum(s, axis, n):
     tile = jnp.broadcast_to(s.astype(jnp.float32), (8, 128))
     return allreduce(tile, axis, n)[0, 0]
@@ -405,16 +551,19 @@
     hidden = jnp.tanh(pre)
     slope = 1.0 - hidden * hidden
 
-    def head_total(part):
-        local = jnp.dot(part, w_head, preferred_element_type=jnp.float32)
-        shape = local.shape
+    def to_flat(local):
         flat = local.reshape(-1, 128)
         lanes = flat.shape[0]
         tall = -(-lanes // (8 * param_count)) * 8 * param_count
-        flat = jnp.pad(flat, ((0, tall - lanes), (0, 0)))
-        return allreduce(flat, "param", param_count)[:lanes].reshape(shape)
-
-    mean = base_mean + head_total(hidden.astype(jnp.bfloat16))
+        return jnp.pad(flat, ((0, tall - lanes), (0, 0)))
+
+    def head_total(part, tile=None, ivflat=None):
+        local = jnp.dot(part, w_head, preferred_element_type=jnp.float32)
+        res = head_allreduce(to_flat(local), param_count, dp_count, tile, ivflat)
+        lanes = local.size // 128
+        return (res[0][:lanes].reshape(local.shape),) + tuple(res[1:])
+
+    mean = base_mean + head_total(hidden.astype(jnp.bfloat16))[0]
     delta = advantages[:, None] * (actions - mean) * inv_var
     head_t = w_head.astype(jnp.float32).T
 
@@ -430,13 +579,16 @@
         return jnp.dot(features, vector_b, preferred_element_type=jnp.float32)
 
     block = width // dp_count
-    grad, direction_b, rr = cg_step("first", dp_count, param_count, block, rowsum(pull(delta)))
+    grad, direction_b, rr_part = cg_step("first", dp_count, param_count, block, rowsum(pull(delta)))
     direction = grad
     resid = grad
     solution = jnp.zeros_like(grad)
     for turn in range(ITERS):
         change = expand(direction_b)
-        dmu = head_total((change * slope).astype(jnp.bfloat16))
+        if turn == 0:
+            dmu, rr = head_total((change * slope).astype(jnp.bfloat16), tile=rr_part)
+        else:
+            (dmu,) = head_total((change * slope).astype(jnp.bfloat16))
         partial = rowsum(pull(dmu * inv_var))
         if turn + 1 < ITERS:
             solution, resid, direction, direction_b, rr = cg_step(
@@ -448,8 +600,9 @@
             )
     moved = expand(moved_b)
     shift = (jnp.tanh(pre + moved) - hidden).astype(jnp.bfloat16)
-    dmean = head_total(shift)
-    kl_value = scalar_sum(jnp.sum(dmean * dmean * inv_var) / (2.0 * batch), "dp", dp_count)
+    ivflat = to_flat(jnp.broadcast_to(inv_var, (rows, inv_var.shape[0])))
+    _, kl_tile = head_total(shift, ivflat=ivflat)
+    kl_value = kl_tile[0, 0] / (2.0 * batch)
     return (step_unit, kl_value / TRIAL_KL)
 
 

time: 377 us -> 358 us (0.950)
  Pallas kernels: 324 us -> 307 us
    pallas_call x3, Pallas kernels: 221 us -> 200 us  [cg_step(): pl.pallas_call(functools.partial(_cg_kernel, mode, n_dp, n_pa), out_shape...]
    pallas_call x5 -> x4, Pallas kernels: 103 us -> 108 us  [head_allreduce(): pl.pallas_call(functools.partial(_head_kernel, n, n_dp, extra, kl), out_s...]
where the time goes in v4:
time: 358 us; the launch traced here: 357 us
  Pallas kernels  307 us (86%)
  matrix products  31.7 us (9%)
  local copies, waits for them, and re-layouts  14.8 us (4%)
    pallas_call x3, Pallas kernels, cg_step(): pl.pallas_call(functools.partial(_cg_kernel, mode, n_dp, n_pa), out_shape...  200 us
    pallas_call x4, Pallas kernels, head_allreduce(): pl.pallas_call(functools.partial(_head_kernel, n, n_dp, extra, kl), out_s...  108 us
    dot_general x3, matrix products, rowsum(): lax.dot_general(features, grads, (((0,), (0,)), ((), ())), preferred_elem...  14.7 us
    dot_general x4, matrix products, head_total(): local = jnp.dot(part, w_head, preferred_element_type=jnp.float32)  11.4 us

profile of v4, /device:TPU:1, one launch (start us, length us, event | category | flops | bytes accessed | tf_op | source)
XLA Modules:
  0.0 356.7 jit_solution(11866353061588544992)
XLA Ops:
  0.6 0.0 copy-start
  0.6 0.0 copy-start.1
  0.7 0.0 copy-start.6
  0.7 0.0 copy-start.3
  0.7 0.0 copy-start.2
  0.7 1.0 copy-done
  1.7 0.0 copy-start.5
  1.7 3.4 fusion.31
  5.1 0.0 copy-done.1
  5.1 0.2 fusion.18
  5.4 0.4 reshape.32
  5.8 0.7 pad.16.refs_0_
  6.5 25.7 %head_allreduce_00.2 = f32[384,128]{1,0:T(8,128)} custom-call(f32[384,128]{1,0:T(8,128)} %pad.16.refs_0_), custom_call_target="tpu_custom_call" | custom-call | tf_op jit(solution)/shard_map/head_allreduce_00/pallas_call | solution.py:526
  32.2 0.9 slice.12
  33.1 0.6 reshape.33
  33.8 0.2 copy.30
  34.0 0.0 copy-done.6
  34.0 0.0 copy-done.3
  34.0 0.0 copy-done.2
  34.0 0.0 copy-done.5
  34.0 0.7 fusion.11
  34.7 4.9 %convolution_bitcast_fusion.2.refs_0_ = f32[2048,128]{1,0:T(8,128)} fusion(bf16[1024,128]{1,0:T(8,128)(2,1)S(1)} %fusion.11, bf16[1024,2048]{1,0:T(8,128)(2,1)} %param.7), kind=kOutput, calls=%fused_computation.2 | convolution fusion | flops 536870912 | bytes 5505024 | tf_op jit(solution)/shard_map/dot_general | solution.py:574
  39.6 60.7 %cg_first.1 = (f32[2048,128]{1,0:T(8,128)}, bf16[2048,128]{1,0:T(8,128)(2,1)}, f32[8,128]{1,0:T(8,128)}) custom-call(f32[2048,128]{1,0:T(8,128)} %convolution_bitcast_fusion.2.refs_0_), custom_call_target="tpu_custom_call" | custom-call | tf_op jit(solution)/shard_map/cg_first/pallas_call | solution.py:395
  100.3 3.7 %fusion.15 = f32[1024,36]{1,0:T(8,128)S(1)} fusion(bf16[128,36]{0,1:T(8,128)(2,1)S(1)} %copy-done.1, bf16[1024,2048]{1,0:T(8,128)(2,1)} %param.7, bf16[2048,128]{1,0:T(8,128)(2,1)} %get-tuple-element.15, f32[1024,128]{1,0:T(8,128)S(1)} %fusion.31), kind=kOutput, calls=%fused_computation.24 | convolution fusion | flops 546832384 | bytes 5399552 | tf_op jit(solution)/shard_map/dot_general | solution.py:561
  104.0 0.4 reshape.34
  104.5 0.7 pad.17.refs_0_
  105.2 27.0 %head_allreduce_10.1 = (f32[384,128]{1,0:T(8,128)}, f32[8,128]{1,0:T(8,128)}) custom-call(f32[384,128]{1,0:T(8,128)} %pad.17.refs_0_, f32[8,128]{1,0:T(8,128)} %get-tuple-element.16.refs_1_), custom_call_target="tpu_custom_call" | custom-call | tf_op jit(solution)/shard_map/head_allreduce_10/pallas_call | solution.py:526
  132.2 0.9 slice.13
  133.1 0.6 reshape.35
  133.7 0.2 copy.34
  133.9 0.7 fusion.10
  134.6 4.9 %convolution_bitcast_fusion.1.refs_0_ = f32[2048,128]{1,0:T(8,128)} fusion(bf16[1024,128]{1,0:T(8,128)(2,1)S(1)} %fusion.10, bf16[1024,2048]{1,0:T(8,128)(2,1)} %param.7), kind=kOutput, calls=%fused_computation.1 | convolution fusion | flops 536870912 | bytes 5505024 | tf_op jit(solution)/shard_map/dot_general | solution.py:574
  139.5 1.1 broadcast_in_dim.2.refs_3_
  140.6 69.1 %cg_iter.1 = (f32[2048,128]{1,0:T(8,128)}, f32[2048,128]{1,0:T(8,128)}, f32[2048,128]{1,0:T(8,128)}, bf16[2048,128]{1,0:T(8,128)(2,1)}, f32[8,128]{1,0:T(8,128)}) custom-call(f32[2048,128]{1,0:T(8,128)} %convolution_bitcast_fusion.1.refs_0_, f32[2048,128]{1,0:T(8,128)} %get-tuple-element.18.refs_1_.refs_2_.refs_5_, ...), custom_call_target="tpu_custom_call" | custom-call | tf_op jit(solution)/shard_map/cg_iter/pallas_call | solution.py:395
  209.7 3.7 %fusion.14 = f32[1024,36]{1,0:T(8,128)S(1)} fusion(bf16[128,36]{0,1:T(8,128)(2,1)S(1)} %copy-done.1, bf16[1024,2048]{1,0:T(8,128)(2,1)} %param.7, bf16[2048,128]{1,0:T(8,128)(2,1)} %get-tuple-element.20, f32[1024,128]{1,0:T(8,128)S(1)} %fusion.31), kind=kOutput, calls=%fused_computation.23 | convolution fusion | flops 546832384 | bytes 5399552 | tf_op jit(solution)/shard_map/dot_general | solution.py:561
  213.5 0.4 reshape.36
  213.9 0.7 pad.18.refs_0_
  214.6 22.4 %head_allreduce_00.3 = f32[384,128]{1,0:T(8,128)} custom-call(f32[384,128]{1,0:T(8,128)} %pad.18.refs_0_), custom_call_target="tpu_custom_call" | custom-call | tf_op jit(solution)/shard_map/head_allreduce_00/pallas_call | solution.py:526
  237.1 0.9 slice.14
  238.0 0.6 reshape.37
  238.6 0.2 copy.38
  238.8 0.7 fusion.9
  239.5 4.9 %convolution_bitcast_fusion.refs_0_ = f32[2048,128]{1,0:T(8,128)} fusion(bf16[1024,128]{1,0:T(8,128)(2,1)S(1)} %fusion.9, bf16[1024,2048]{1,0:T(8,128)(2,1)} %param.7), kind=kOutput, calls=%fused_computation | convolution fusion | flops 536870912 | bytes 5505024 | tf_op jit(solution)/shard_map/dot_general | solution.py:574
  244.4 69.8 %cg_last.1 = (f32[64,128]{1,0:T(8,128)}, bf16[2048,128]{1,0:T(8,128)(2,1)}) custom-call(f32[2048,128]{1,0:T(8,128)} %convolution_bitcast_fusion.refs_0_, f32[2048,128]{1,0:T(8,128)} %get-tuple-element.21.refs_1_, f32[2048,128]{1,0:T(8,128)} %get-tuple-element.22.refs_2_, f32[2048,128]{1,0:T(8,128)} %get-tuple-element.23.refs_3_, ...), custom_call_target="tpu_custom_call" | custom-call | tf_op jit(solution)/shard_map/cg_last/pallas_call | solution.py:395
  314.2 0.0 copy-start.4
  314.2 3.8 %fusion.16 = f32[1024,36]{1,0:T(8,128)S(1)} fusion(bf16[128,36]{0,1:T(8,128)(2,1)S(1)} %copy-done.1, f32[1024,128]{1,0:T(8,128)S(1)} %fusion.31, bf16[1024,2048]{1,0:T(8,128)(2,1)} %param.7, bf16[2048,128]{1,0:T(8,128)(2,1)} %get-tuple-element.26), kind=kOutput, calls=%fused_computation.25 | convolution fusion | flops 546701312 | bytes 5399552 | tf_op jit(solution)/shard_map/dot_general | solution.py:561
  318.0 0.4 reshape.38
  318.4 0.7 pad.19.refs_0_
  319.2 0.4 reshape.39
  319.6 0.7 pad.20.refs_1_
  320.3 32.8 %head_allreduce_01.1 = (f32[384,128]{1,0:T(8,128)}, f32[8,128]{1,0:T(8,128)}) custom-call(f32[384,128]{1,0:T(8,128)} %pad.19.refs_0_, f32[384,128]{1,0:T(8,128)} %pad.20.refs_1_), custom_call_target="tpu_custom_call" | custom-call | tf_op jit(solution)/shard_map/head_allreduce_01/pallas_call | solution.py:526
  353.1 1.2 slice.15
  354.9 0.0 copy-done.4
  354.9 0.6 copy.54
  (2 shorter events, 0.0 us)
Async XLA Ops:
  0.6 1.0 copy-start
  0.6 4.5 %copy-start.1 = (bf16[128,36]{0,1:T(8,128)(2,1)S(1)}, bf16[128,36]{0,1:T(8,128)(2,1)}, u32[]{:S(2)}) copy-start(bf16[128,36]{0,1:T(8,128)(2,1)} %param.9) | copy-start | bytes 27652
  0.7 33.3 %copy-start.6 = (f32[36]{0:T(128)S(1)}, f32[36]{0:T(128)}, u32[]{:S(2)}) copy-start(f32[36]{0:T(128)} %param.13) | copy-start | bytes 436
  0.7 33.3 %copy-start.3 = (f32[1024,36]{0,1:T(8,128)S(1)}, f32[1024,36]{0,1:T(8,128)}, u32[]{:S(2)}) copy-start(f32[1024,36]{0,1:T(8,128)} %param.10) | copy-start | bytes 442372
  0.7 33.3 %copy-start.2 = (f32[1024,36]{0,1:T(8,128)S(1)}, f32[1024,36]{0,1:T(8,128)}, u32[]{:S(2)}) copy-start(f32[1024,36]{0,1:T(8,128)} %param.11) | copy-start | bytes 442372
  1.7 32.3 %copy-start.5 = (f32[1024]{0:T(1024)S(1)}, f32[1024]{0:T(1024)}, u32[]{:S(2)}) copy-start(f32[1024]{0:T(1024)} %param.12) | copy-start | bytes 12292
  314.2 40.7 %copy-start.4 = (f32[64,128]{1,0:T(8,128)S(1)}, f32[64,128]{1,0:T(8,128)}, u32[]{:S(2)}) copy-start(f32[64,128]{1,0:T(8,128)} %get-tuple-element.30) | copy-start | bytes 98308

commit v5 on v0

v5 whole, which is shorter than its diff:
```python
import functools

import jax
import jax.numpy as jnp
from jax import lax
from jax.experimental import pallas as pl
from jax.experimental.pallas import tpu as pltpu
from jax.sharding import PartitionSpec as P

D = 2048
UNITS = 2048
ITERS = 2


DAMPING = 0.01
TRIAL_KL = 4.0

MESH = pl.DeviceIdType.MESH
AXES = ("dp", "param")
ACT_PAD = 48
HEAD_ROWS = 24
HIGHEST = lax.Precision.HIGHEST


def _device(axis, partner):
    return tuple(partner if name == axis else lax.axis_index(name) for name in AXES)


def _tile_sum(x):
    return jnp.sum(jnp.sum(x, axis=0, keepdims=True), axis=1, keepdims=True)


def _scratch_plan(n_dp, n_pa, rows, width, units, iters):
    f32, bf16 = jnp.float32, jnp.bfloat16
    groups = n_pa // (ACT_PAD // HEAD_ROWS)
    lanes = rows // groups
    dma = pltpu.SemaphoreType.DMA(())
    plan = [
        ("pre", pltpu.VMEM((rows, units), f32)),
        ("hid", pltpu.VMEM((rows, units), f32)),
        ("slope", pltpu.VMEM((rows, units), f32)),
        ("gb", pltpu.VMEM((rows, units), bf16)),
        ("chg", pltpu.VMEM((rows, units), f32)),
        ("part", pltpu.VMEM((width, units), f32)),
        ("grad", pltpu.VMEM((width, units), f32)),
        ("x", pltpu.VMEM((width, units), f32)),
        ("r", pltpu.VMEM((width, units), f32)),
        ("p", pltpu.VMEM((width, units), f32)),
        ("pb", pltpu.VMEM((width, units), bf16)),
    ]
    for h in range(iters + 2):
        plan += [
            (f"hloc{h}", pltpu.VMEM((ACT_PAD, rows), f32)),
            (f"hrecv{h}", pltpu.VMEM((n_pa, HEAD_ROWS, lanes), f32)),
            (f"hgat{h}", pltpu.VMEM((ACT_PAD, rows), f32)),
        ] + [(f"hsem{h}_{i}", dma) for i in range(4)]
    for d in range(iters + 1):
        plan += [
            (f"drecv{d}", pltpu.VMEM((n_dp, width // n_dp, units), f32)),
            (f"dgat{d}", pltpu.VMEM((width, units), f32)),
        ] + [(f"dsem{d}_{i}", dma) for i in range(4)]
    for k in range(iters + 1):
        plan += [
            (f"stile{k}", pltpu.VMEM((8, 128), f32)),
            (f"srecv{k}", pltpu.VMEM((n_pa, 8, 128), f32)),
        ] + [(f"ssem{k}_{i}", dma) for i in range(2)]
    plan += [
        ("ktile", pltpu.VMEM((8, 128), f32)),
        ("krecv", pltpu.VMEM((n_dp, 8, 128), f32)),
        ("ksem0", dma),
        ("ksem1", dma),
    ]
    return plan


def _mega_kernel(names, n_dp, n_pa, iters, batch, *refs):
    (feat, wh, whtb, whtf, bmT, actT, adv, ivT, step_out, kl_out) = refs[:10]
    s = dict(zip(names, refs[10:]))
    rows, width = feat.shape
    units = wh.shape[1]
    groups = n_pa // (ACT_PAD // HEAD_ROWS)
    lanes = rows // groups
    cdp = width // n_dp
    md = lax.axis_index("dp")
    mp = lax.axis_index("param")
    dpeers = [lax.rem(md + j, n_dp) for j in range(1, n_dp)]
    ppeers = [lax.rem(mp + j, n_pa) for j in range(1, n_pa)]

    barrier = pltpu.get_barrier_semaphore()
    for p in dpeers:
        pl.semaphore_signal(barrier, inc=1, device_id=_device("dp", p), device_id_type=MESH)
    for p in ppeers:
        pl.semaphore_signal(barrier, inc=1, device_id=_device("param", p), device_id_type=MESH)
    pl.semaphore_wait(barrier, len(dpeers) + len(ppeers))

    def wait_all(buf, count, send_sem, recv_sem, axis):
        cp = pltpu.make_async_remote_copy(
            src_ref=buf.at[pl.ds(0, count)],
            dst_ref=buf.at[pl.ds(0, count)],
            send_sem=send_sem,
            recv_sem=recv_sem,
            device_id=_device(axis, lax.axis_index(axis)),
            device_id_type=MESH,
        )
        cp.wait_send()
        cp.wait_recv()

    def send(src, dst, send_sem, recv_sem, axis, peer):
        pltpu.make_async_remote_copy(
            src_ref=src, dst_ref=dst, send_sem=send_sem, recv_sem=recv_sem,
            device_id=_device(axis, peer), device_id_type=MESH,
        ).start()

    def hchunk(buf, k):
        r0 = pl.multiple_of((k // groups) * HEAD_ROWS, 8)
        l0 = pl.multiple_of(lax.rem(k, groups) * lanes, 128)
        return buf.at[pl.ds(r0, HEAD_ROWS), pl.ds(l0, lanes)]

    def head_allreduce(h, extra=None):
        loc, recv, gat = s[f"hloc{h}"], s[f"hrecv{h}"], s[f"hgat{h}"]
        sa, ra, sb, rb = (s[f"hsem{h}_{i}"] for i in range(4))
        for p in ppeers:
            send(hchunk(loc, p), recv.at[mp], sa, ra, "param", p)
        if extra is not None:
            tile, erecv = s[f"stile{extra}"], s[f"srecv{extra}"]
            es, er = s[f"ssem{extra}_0"], s[f"ssem{extra}_1"]
            for p in ppeers:
                send(tile, erecv.at[mp], es, er, "param", p)
        wait_all(recv, n_pa - 1, sa, ra, "param")
        recv[mp] = hchunk(loc, mp)[...]
        acc = recv[0]
        for i in range(1, n_pa):
            acc = acc + recv[i]
        hchunk(gat, mp)[...] = acc
        for p in ppeers:
            send(hchunk(gat, mp), hchunk(gat, mp), sb, rb, "param", p)
        total = None
        if extra is not None:
            wait_all(erecv, n_pa - 1, es, er, "param")
            erecv[mp] = tile[...]
            total = erecv[0]
            for i in range(1, n_pa):
                total = total + erecv[i]
        wait_all(recv, n_pa - 1, sb, rb, "param")
        return total

    def dp_allreduce(d):
        recv, gat = s[f"drecv{d}"], s[f"dgat{d}"]
        sa, ra, sb, rb = (s[f"dsem{d}_{i}"] for i in range(4))
        part = s["part"]
        for p in dpeers:
            send(part.at[pl.ds(pl.multiple_of(p * cdp, 8), cdp)], recv.at[md], sa, ra, "dp", p)
        wait_all(recv, n_dp - 1, sa, ra, "dp")
        mine = pl.ds(pl.multiple_of(md * cdp, 8), cdp)
        recv[md] = part[mine]
        acc = recv[0]
        for i in range(1, n_dp):
            acc = acc + recv[i]
        gat[mine] = acc
        for p in dpeers:
            send(gat.at[mine], gat.at[mine], sb, rb, "dp", p)
        wait_all(recv, n_dp - 1, sb, rb, "dp")
        return gat

    def param_round(k, values):
        tile, recv = s[f"stile{k}"], s[f"srecv{k}"]
        ss, sr = s[f"ssem{k}_0"], s[f"ssem{k}_1"]
        row = lax.broadcasted_iota(jnp.int32, (8, 128), 0)
        t = jnp.zeros((8, 128), jnp.float32)
        for i, v in enumerate(values):
            t = jnp.where(row == i, jnp.broadcast_to(v, (8, 128)), t)
        tile[...] = t
        for p in ppeers:
            send(tile, recv.at[mp], ss, sr, "param", p)
        wait_all(recv, n_pa - 1, ss, sr, "param")
        recv[mp] = tile[...]
        total = recv[0]
        for i in range(1, n_pa):
            total = total + recv[i]
        return [total[i:i + 1, 0:1] for i in range(len(values))]

    def expand(vec_b, out):
        blk = min(256, rows)

        def body(i, carry):
            r0 = pl.multiple_of(i * blk, blk)
            out[pl.ds(r0, blk), :] = jnp.dot(feat[pl.ds(r0, blk), :], vec_b[...], preferred_element_type=jnp.float32)
            return carry

        lax.fori_loop(0, rows // blk, body, 0)

    def rowsum(g):
        part = s["part"]
        blk = min(256, width)

        def body(i, carry):
            c0 = pl.multiple_of(i * blk, blk)
            part[pl.ds(c0, blk), :] = lax.dot_general(
                feat[:, pl.ds(c0, blk)], g[...], (((0,), (0,)), ((), ())), preferred_element_type=jnp.float32
            )
            return carry

        lax.fori_loop(0, width // blk, body, 0)

    def head_local(h, vals_b):
        s[f"hloc{h}"][...] = lax.dot_general(
            whtb[...], vals_b, (((1,), (1,)), ((), ())), preferred_element_type=jnp.float32
        )

    def pull(momentT):
        gb = s["gb"]
        prod = lax.dot_general(momentT, whtf[...], (((0,), (0,)), ((), ())), precision=HIGHEST,
                               preferred_element_type=jnp.float32)
        gb[...] = (prod * s["slope"][...] / batch).astype(jnp.bfloat16)
        return gb

    expand(wh, s["pre"])
    hidden = jnp.tanh(s["pre"][...])
    s["hid"][...] = hidden
    s["slope"][...] = 1.0 - hidden * hidden
    head_local(0, hidden.astype(jnp.bfloat16))
    head_allreduce(0)
    meanT = bmT[...] + s["hgat0"][...]
    deltaT = adv[...] * (actT[...] - meanT) * ivT[...]
    rowsum(pull(deltaT))
    grad = dp_allreduce(0)[...]
    s["grad"][...] = grad
    s["r"][...] = grad
    s["p"][...] = grad
    s["x"][...] = jnp.zeros_like(grad)
    s["pb"][...] = grad.astype(jnp.bfloat16)
    s["stile0"][...] = jnp.broadcast_to(_tile_sum(grad * grad), (8, 128))
    rr = None
    for t in range(iters):
        expand(s["pb"], s["chg"])
        dh = (s["chg"][...] * s["slope"][...]).astype(jnp.bfloat16)
        head_local(t + 1, dh)
        total = head_allreduce(t + 1, extra=0 if t == 0 else None)
        if t == 0:
            rr = total[0:1, 0:1]
        rowsum(pull(s[f"hgat{t + 1}"][...] * ivT[...]))
        direction = s["p"][...]
        resid = s["r"][...]
        image = dp_allreduce(t + 1)[...] + DAMPING * direction
        if t + 1 < iters:
            curv, r_img, img_img = param_round(
                t + 1, [_tile_sum(direction * image), _tile_sum(resid * image), _tile_sum(image * image)]
            )
            alpha = rr / curv
            s["x"][...] = s["x"][...] + alpha * direction
            r_new = resid - alpha * image
            s["r"][...] = r_new
            rr_next = rr - 2.0 * alpha * r_img + alpha * alpha * img_img
            p_new = r_new + rr_next / rr * direction
            s["p"][...] = p_new
            s["pb"][...] = p_new.astype(jnp.bfloat16)
            rr = rr_next
        else:
            sol = s["x"][...]
            gap = s["grad"][...] - resid
            curv, x_gap, x_img, p_gap = param_round(
                t + 1,
                [_tile_sum(direction * image), _tile_sum(sol * gap), _tile_sum(sol * image), _tile_sum(direction * gap)],
            )
            alpha = rr / curv
            x_new = sol + alpha * direction
            shs = x_gap + alpha * (x_img + p_gap) + alpha * alpha * curv
            s["x"][...] = x_new
            blk = step_out.shape[0]
            step_out[...] = s["x"][pl.ds(pl.multiple_of(md * blk, 8), blk)] * jnp.sqrt(D * UNITS / shs)
            reach = jnp.sqrt(2.0 * TRIAL_KL / shs)
            s["pb"][...] = (reach * x_new).astype(jnp.bfloat16)
    expand(s["pb"], s["chg"])
    shift = (jnp.tanh(s["pre"][...] + s["chg"][...]) - s["hid"][...]).astype(jnp.bfloat16)
    last = iters + 1
    head_local(last, shift)
    head_allreduce(last)
    dmeanT = s[f"hgat{last}"][...]
    ktile, krecv = s["ktile"], s["krecv"]
    ktile[...] = jnp.broadcast_to(_tile_sum(dmeanT * dmeanT * ivT[...]), (8, 128))
    for p in dpeers:
        send(ktile, krecv.at[md], s["ksem0"], s["ksem1"], "dp", p)
    wait_all(krecv, n_dp - 1, s["ksem0"], s["ksem1"], "dp")
    krecv[md] = ktile[...]
    ktot = krecv[0]
    for i in range(1, n_dp):
        ktot = ktot + krecv[i]
    kl_out[...] = ktot / (2.0 * batch) / TRIAL_KL


def shards(features, w_hidden, w_head, base_mean, actions, advantages, log_std):
    rows, width = features.shape
    units = w_hidden.shape[1]
    act = w_head.shape[1]
    dp_count = lax.axis_size("dp")
    param_count = lax.axis_size("param")
    batch = rows * dp_count
    inv_var = jnp.exp(-2.0 * log_std)
    padT = lambda a: jnp.pad(a.T, ((0, ACT_PAD - act), (0, 0)))
    whtb = padT(w_head)
    whtf = whtb.astype(jnp.float32)
    bmT = padT(base_mean)
    actT = padT(actions)
    ivT = jnp.pad(jnp.broadcast_to(inv_var[:, None], (act, rows)), ((0, ACT_PAD - act), (0, 0)))
    adv = advantages.reshape(1, rows)
    plan = _scratch_plan(dp_count, param_count, rows, width, units, ITERS)
    names = [name for name, _ in plan]
    vspec = pl.BlockSpec(memory_space=pltpu.VMEM)
    block = width // dp_count
    step_unit, kl_tile = pl.pallas_call(
        functools.partial(_mega_kernel, names, dp_count, param_count, ITERS, batch),
        out_shape=(jax.ShapeDtypeStruct((block, units), jnp.float32), jax.ShapeDtypeStruct((8, 128), jnp.float32)),
        in_specs=[vspec] * 8,
        out_specs=(vspec, vspec),
        scratch_shapes=[spec for _, spec in plan],
        compiler_params=pltpu.CompilerParams(collective_id=0, has_side_effects=True, vmem_limit_bytes=60 * 1024 * 1024),
        name="trust_region_step",
    )(features, w_hidden, whtb, whtf, bmT, actT, adv, ivT)
    return (step_unit, kl_tile[0, 0])


def solution(mesh):
    return jax.shard_map(
        shards,
        mesh=mesh,
        in_specs=(
            P("dp", None),
            P(None, "param"),
            P("param", None),
            P("dp", None),
            P("dp", None),
            P("dp"),
            P(),
        ),
        out_specs=(P("dp", "param"), P()),
        check_vma=False,
    )
```

time: 1150 us -> 288 us (0.25)
  waiting for transfers between devices: 899 us -> 0 us
  Pallas kernels: 0 us -> 278 us
  blocking collectives: 168 us -> 0 us
  matrix products: 34.5 us -> 0 us
  between operations: 22.2 us -> 0.64 us
    psum x7 -> x0, waiting for transfers between devices: 899 us -> none  [the longest x3 466 us: rowsum(): return lax.psum(term, 'dp')]
    pallas_call x0 -> x1, Pallas kernels: none -> 278 us  [shards(): pl.pallas_call(functools.partial(_mega_kernel, names, dp_count, param_cou...]
    psum x5 -> x0, blocking collectives: 168 us -> none  [the longest x4 106 us: total(): return lax.psum((values[0],), 'param')]
    dot_general x11 -> x0, matrix products: 34.5 us -> none  [the longest x4 14.5 us: head_total(): jnp.dot(part, w_head, preferred_element_type=jnp.float32)]
  transfers between devices with their start and end apart: 7 -> 0, of which waited for: 7 -> 0; matrix products, arithmetic and copies ran while one was open for 0% -> 0% of each run, Pallas kernels for 0% -> 0%
where the time goes in v5:
time: 288 us; the launch traced here: 287 us
  Pallas kernels  278 us (97%)
  local copies, waits for them, and re-layouts  6.53 us (2%)
    pallas_call x1, Pallas kernels, shards(): pl.pallas_call(functools.partial(_mega_kernel, names, dp_count, param_cou...  278 us

profile of v5, /device:TPU:1, one launch (start us, length us, event | category | flops | bytes accessed | tf_op | source)
XLA Modules:
  0.0 287.2 jit_solution(13708618388194596846)
XLA Ops:
  0.6 0.7 multiply_exponential_fusion
  1.3 1.3 pad_convert_fusion
  2.6 0.8 pad.20.refs_7_
  3.4 1.6 pad.17.refs_4_
  5.0 1.6 pad.18.refs_5_
  6.6 278.1 %trust_region_step.1 = (f32[64,128]{1,0:T(8,128)}, f32[8,128]{1,0:T(8,128)}) custom-call(bf16[1024,2048]{1,0:T(8,128)(2,1)} %refs_0_.1, bf16[2048,128]{1,0:T(8,128)(2,1)} %refs_1_.1, bf16[48,128]{1,0:T(8,128)(2,1)} %get-tuple-element.7.refs_2_, f32[48,128]{1,0:T(8,128)} %get-tuple-element.6.refs_3_, f32[48,1024]{1,0:T(8,128)} %pad.17.refs_4_, ...), custom_call_target="tpu_custom_call" | custom-call | tf_op jit(solution)/shard_map/trust_region_step/pallas_call | solution.py:310
  284.7 1.2 slice.3
  285.9 1.4 copy.10
  (1 shorter events, 0.0 us)

commit v6 on v5

--- a/solution.py
+++ b/solution.py
@@ -119,13 +119,9 @@
     def head_allreduce(h, extra=None):
         loc, recv, gat = s[f"hloc{h}"], s[f"hrecv{h}"], s[f"hgat{h}"]
         sa, ra, sb, rb = (s[f"hsem{h}_{i}"] for i in range(4))
-        for p in ppeers:
-            send(hchunk(loc, p), recv.at[mp], sa, ra, "param", p)
         if extra is not None:
             tile, erecv = s[f"stile{extra}"], s[f"srecv{extra}"]
             es, er = s[f"ssem{extra}_0"], s[f"ssem{extra}_1"]
-            for p in ppeers:
-                send(tile, erecv.at[mp], es, er, "param", p)
         wait_all(recv, n_pa - 1, sa, ra, "param")
         recv[mp] = hchunk(loc, mp)[...]
         acc = recv[0]
@@ -148,8 +144,6 @@
         recv, gat = s[f"drecv{d}"], s[f"dgat{d}"]
         sa, ra, sb, rb = (s[f"dsem{d}_{i}"] for i in range(4))
         part = s["part"]
-        for p in dpeers:
-            send(part.at[pl.ds(pl.multiple_of(p * cdp, 8), cdp)], recv.at[md], sa, ra, "dp", p)
         wait_all(recv, n_dp - 1, sa, ra, "dp")
         mine = pl.ds(pl.multiple_of(md * cdp, 8), cdp)
         recv[md] = part[mine]
@@ -179,33 +173,44 @@
             total = total + recv[i]
         return [total[i:i + 1, 0:1] for i in range(len(values))]
 
-    def expand(vec_b, out):
-        blk = min(256, rows)
-
-        def body(i, carry):
-            r0 = pl.multiple_of(i * blk, blk)
+    def expand_head(vec_b, out, make_vals, h, extra=None):
+        loc, recv = s[f"hloc{h}"], s[f"hrecv{h}"]
+        sa, ra = s[f"hsem{h}_0"], s[f"hsem{h}_1"]
+        if extra is not None:
+            tile, erecv = s[f"stile{extra}"], s[f"srecv{extra}"]
+            es, er = s[f"ssem{extra}_0"], s[f"ssem{extra}_1"]
+            for p in ppeers:
+                send(tile, erecv.at[mp], es, er, "param", p)
+        blk = max(lanes, 256)
+        for b in range(rows // blk):
+            r0 = b * blk
             out[pl.ds(r0, blk), :] = jnp.dot(feat[pl.ds(r0, blk), :], vec_b[...], preferred_element_type=jnp.float32)
-            return carry
-
-        lax.fori_loop(0, rows // blk, body, 0)
-
-    def rowsum(g):
-        part = s["part"]
-        blk = min(256, width)
-
-        def body(i, carry):
-            c0 = pl.multiple_of(i * blk, blk)
+            vals = make_vals(r0, blk)
+            loc[:, pl.ds(r0, blk)] = lax.dot_general(
+                whtb[...], vals, (((1,), (1,)), ((), ())), preferred_element_type=jnp.float32
+            )
+            for lg in range(r0 // lanes, (r0 + blk) // lanes):
+                for rg in range(ACT_PAD // HEAD_ROWS):
+                    k = rg * groups + lg
+
+                    @pl.when(mp != k)
+                    def _():
+                        send(hchunk(loc, k), recv.at[mp], sa, ra, "param", k)
+
+    def rowsum(g, d):
+        part, recv = s["part"], s[f"drecv{d}"]
+        sa, ra = s[f"dsem{d}_0"], s[f"dsem{d}_1"]
+        blk = max(cdp, min(256, width))
+        for b in range(width // blk):
+            c0 = b * blk
             part[pl.ds(c0, blk), :] = lax.dot_general(
                 feat[:, pl.ds(c0, blk)], g[...], (((0,), (0,)), ((), ())), preferred_element_type=jnp.float32
             )
-            return carry
-
-        lax.fori_loop(0, width // blk, body, 0)
-
-    def head_local(h, vals_b):
-        s[f"hloc{h}"][...] = lax.dot_general(
-            whtb[...], vals_b, (((1,), (1,)), ((), ())), preferred_element_type=jnp.float32
-        )
+            for k in range(c0 // cdp, (c0 + blk) // cdp):
+
+                @pl.when(md != k)
+                def _():
+                    send(part.at[pl.ds(k * cdp, cdp)], recv.at[md], sa, ra, "dp", k)
 
     def pull(momentT):
         gb = s["gb"]
@@ -214,15 +219,25 @@
         gb[...] = (prod * s["slope"][...] / batch).astype(jnp.bfloat16)
         return gb
 
-    expand(wh, s["pre"])
-    hidden = jnp.tanh(s["pre"][...])
-    s["hid"][...] = hidden
-    s["slope"][...] = 1.0 - hidden * hidden
-    head_local(0, hidden.astype(jnp.bfloat16))
+    def hidden_vals(r0, blk):
+        pre = s["pre"][pl.ds(r0, blk), :]
+        hidden = jnp.tanh(pre)
+        s["hid"][pl.ds(r0, blk), :] = hidden
+        s["slope"][pl.ds(r0, blk), :] = 1.0 - hidden * hidden
+        return hidden.astype(jnp.bfloat16)
+
+    def change_vals(r0, blk):
+        return (s["chg"][pl.ds(r0, blk), :] * s["slope"][pl.ds(r0, blk), :]).astype(jnp.bfloat16)
+
+    def shift_vals(r0, blk):
+        moved = jnp.tanh(s["pre"][pl.ds(r0, blk), :] + s["chg"][pl.ds(r0, blk), :])
+        return (moved - s["hid"][pl.ds(r0, blk), :]).astype(jnp.bfloat16)
+
+    expand_head(wh, s["pre"], hidden_vals, 0)
     head_allreduce(0)
     meanT = bmT[...] + s["hgat0"][...]
     deltaT = adv[...] * (actT[...] - meanT) * ivT[...]
-    rowsum(pull(deltaT))
+    rowsum(pull(deltaT), 0)
     grad = dp_allreduce(0)[...]
     s["grad"][...] = grad
     s["r"][...] = grad
@@ -232,13 +247,11 @@
     s["stile0"][...] = jnp.broadcast_to(_tile_sum(grad * grad), (8, 128))
     rr = None
     for t in range(iters):
-        expand(s["pb"], s["chg"])
-        dh = (s["chg"][...] * s["slope"][...]).astype(jnp.bfloat16)
-        head_local(t + 1, dh)
+        expand_head(s["pb"], s["chg"], change_vals, t + 1, extra=0 if t == 0 else None)
         total = head_allreduce(t + 1, extra=0 if t == 0 else None)
         if t == 0:
             rr = total[0:1, 0:1]
-        rowsum(pull(s[f"hgat{t + 1}"][...] * ivT[...]))
+        rowsum(pull(s[f"hgat{t + 1}"][...] * ivT[...]), t + 1)
         direction = s["p"][...]
         resid = s["r"][...]
         image = dp_allreduce(t + 1)[...] + DAMPING * direction
@@ -270,10 +283,8 @@
             step_out[...] = s["x"][pl.ds(pl.multiple_of(md * blk, 8), blk)] * jnp.sqrt(D * UNITS / shs)
             reach = jnp.sqrt(2.0 * TRIAL_KL / shs)
             s["pb"][...] = (reach * x_new).astype(jnp.bfloat16)
-    expand(s["pb"], s["chg"])
-    shift = (jnp.tanh(s["pre"][...] + s["chg"][...]) - s["hid"][...]).astype(jnp.bfloat16)
     last = iters + 1
-    head_local(last, shift)
+    expand_head(s["pb"], s["chg"], shift_vals, last)
     head_allreduce(last)
     dmeanT = s[f"hgat{last}"][...]
     ktile, krecv = s["ktile"], s["krecv"]

time: 288 us -> 280 us (0.972)
  Pallas kernels: 278 us -> 269 us
    pallas_call x1, Pallas kernels: 278 us -> 269 us  [shards(): pl.pallas_call(functools.partial(_mega_kernel, names, dp_count, param_cou...]
where the time goes in v6:
time: 280 us; the launch traced here: 279 us
  Pallas kernels  269 us (96%)
  local copies, waits for them, and re-layouts  6.53 us (2%)
    pallas_call x1, Pallas kernels, shards(): pl.pallas_call(functools.partial(_mega_kernel, names, dp_count, param_cou...  269 us

profile of v6, /device:TPU:1, one launch (start us, length us, event | category | flops | bytes accessed | tf_op | source)
XLA Modules:
  0.0 278.6 jit_solution(8730430687005069354)
XLA Ops:
  0.6 0.7 multiply_exponential_fusion
  1.3 1.3 pad_convert_fusion
  2.6 0.8 pad.20.refs_7_
  3.4 1.6 pad.17.refs_4_
  5.0 1.6 pad.18.refs_5_
  6.6 269.4 %trust_region_step.1 = (f32[64,128]{1,0:T(8,128)}, f32[8,128]{1,0:T(8,128)}) custom-call(bf16[1024,2048]{1,0:T(8,128)(2,1)} %refs_0_.1, bf16[2048,128]{1,0:T(8,128)(2,1)} %refs_1_.1, bf16[48,128]{1,0:T(8,128)(2,1)} %get-tuple-element.7.refs_2_, f32[48,128]{1,0:T(8,128)} %get-tuple-element.6.refs_3_, f32[48,1024]{1,0:T(8,128)} %pad.17.refs_4_, ...), custom_call_target="tpu_custom_call" | custom-call | tf_op jit(solution)/shard_map/trust_region_step/pallas_call | solution.py:321
  276.0 1.2 slice.3
  277.2 1.4 copy.10
  (1 shorter events, 0.0 us)

commit v7 on v6

--- a/solution.py
+++ b/solution.py
@@ -54,7 +54,7 @@
             (f"hrecv{h}", pltpu.VMEM((n_pa, HEAD_ROWS, lanes), f32)),
             (f"hgat{h}", pltpu.VMEM((ACT_PAD, rows), f32)),
         ] + [(f"hsem{h}_{i}", dma) for i in range(4)]
-    for d in range(iters + 1):
+    for d in range(iters):
         plan += [
             (f"drecv{d}", pltpu.VMEM((n_dp, width // n_dp, units), f32)),
             (f"dgat{d}", pltpu.VMEM((width, units), f32)),
@@ -65,6 +65,10 @@
             (f"srecv{k}", pltpu.VMEM((n_pa, 8, 128), f32)),
         ] + [(f"ssem{k}_{i}", dma) for i in range(2)]
     plan += [
+        ("ltile", pltpu.VMEM((8, 128), f32)),
+        ("lrecv", pltpu.VMEM((n_dp, 8, 128), f32)),
+        ("lsem0", dma),
+        ("lsem1", dma),
         ("ktile", pltpu.VMEM((8, 128), f32)),
         ("krecv", pltpu.VMEM((n_dp, 8, 128), f32)),
         ("ksem0", dma),
@@ -91,7 +95,6 @@
         pl.semaphore_signal(barrier, inc=1, device_id=_device("dp", p), device_id_type=MESH)
     for p in ppeers:
         pl.semaphore_signal(barrier, inc=1, device_id=_device("param", p), device_id_type=MESH)
-    pl.semaphore_wait(barrier, len(dpeers) + len(ppeers))
 
     def wait_all(buf, count, send_sem, recv_sem, axis):
         cp = pltpu.make_async_remote_copy(
@@ -156,7 +159,7 @@
         wait_all(recv, n_dp - 1, sb, rb, "dp")
         return gat
 
-    def param_round(k, values):
+    def param_start(k, values):
         tile, recv = s[f"stile{k}"], s[f"srecv{k}"]
         ss, sr = s[f"ssem{k}_0"], s[f"ssem{k}_1"]
         row = lax.broadcasted_iota(jnp.int32, (8, 128), 0)
@@ -166,14 +169,22 @@
         tile[...] = t
         for p in ppeers:
             send(tile, recv.at[mp], ss, sr, "param", p)
+
+    def param_finish(k, count):
+        tile, recv = s[f"stile{k}"], s[f"srecv{k}"]
+        ss, sr = s[f"ssem{k}_0"], s[f"ssem{k}_1"]
         wait_all(recv, n_pa - 1, ss, sr, "param")
         recv[mp] = tile[...]
         total = recv[0]
         for i in range(1, n_pa):
             total = total + recv[i]
-        return [total[i:i + 1, 0:1] for i in range(len(values))]
-
-    def expand_head(vec_b, out, make_vals, h, extra=None):
+        return [total[i:i + 1, 0:1] for i in range(count)]
+
+    def param_round(k, values):
+        param_start(k, values)
+        return param_finish(k, len(values))
+
+    def expand_head(vec_b, out, make_vals, h, extra=None, entry=False):
         loc, recv = s[f"hloc{h}"], s[f"hrecv{h}"]
         sa, ra = s[f"hsem{h}_0"], s[f"hsem{h}_1"]
         if extra is not None:
@@ -189,6 +200,8 @@
             loc[:, pl.ds(r0, blk)] = lax.dot_general(
                 whtb[...], vals, (((1,), (1,)), ((), ())), preferred_element_type=jnp.float32
             )
+            if entry:
+                continue
             for lg in range(r0 // lanes, (r0 + blk) // lanes):
                 for rg in range(ACT_PAD // HEAD_ROWS):
                     k = rg * groups + lg
@@ -196,16 +209,22 @@
                     @pl.when(mp != k)
                     def _():
                         send(hchunk(loc, k), recv.at[mp], sa, ra, "param", k)
-
-    def rowsum(g, d):
-        part, recv = s["part"], s[f"drecv{d}"]
-        sa, ra = s[f"dsem{d}_0"], s[f"dsem{d}_1"]
+        if entry:
+            pl.semaphore_wait(barrier, len(dpeers) + len(ppeers))
+            for p in ppeers:
+                send(hchunk(loc, p), recv.at[mp], sa, ra, "param", p)
+
+    def rowsum(g, d=None):
+        part = s["part"]
         blk = max(cdp, min(256, width))
         for b in range(width // blk):
             c0 = b * blk
             part[pl.ds(c0, blk), :] = lax.dot_general(
                 feat[:, pl.ds(c0, blk)], g[...], (((0,), (0,)), ((), ())), preferred_element_type=jnp.float32
             )
+            if d is None:
+                continue
+            recv, sa, ra = s[f"drecv{d}"], s[f"dsem{d}_0"], s[f"dsem{d}_1"]
             for k in range(c0 // cdp, (c0 + blk) // cdp):
 
                 @pl.when(md != k)
@@ -233,7 +252,7 @@
         moved = jnp.tanh(s["pre"][pl.ds(r0, blk), :] + s["chg"][pl.ds(r0, blk), :])
         return (moved - s["hid"][pl.ds(r0, blk), :]).astype(jnp.bfloat16)
 
-    expand_head(wh, s["pre"], hidden_vals, 0)
+    expand_head(wh, s["pre"], hidden_vals, 0, entry=True)
     head_allreduce(0)
     meanT = bmT[...] + s["hgat0"][...]
     deltaT = adv[...] * (actT[...] - meanT) * ivT[...]
@@ -251,9 +270,40 @@
         total = head_allreduce(t + 1, extra=0 if t == 0 else None)
         if t == 0:
             rr = total[0:1, 0:1]
-        rowsum(pull(s[f"hgat{t + 1}"][...] * ivT[...]), t + 1)
+        rowsum(pull(s[f"hgat{t + 1}"][...] * ivT[...]), t + 1 if t + 1 < iters else None)
         direction = s["p"][...]
         resid = s["r"][...]
+        if t + 1 == iters:
+            part = s["part"][...]
+            sol = s["x"][...]
+            row = lax.broadcasted_iota(jnp.int32, (8, 128), 0)
+            lt = jnp.where(row == 0, jnp.broadcast_to(_tile_sum(direction * part), (8, 128)),
+                           jnp.broadcast_to(_tile_sum(sol * part), (8, 128)))
+            s["ltile"][...] = lt
+            for p in dpeers:
+                send(s["ltile"], s["lrecv"].at[md], s["lsem0"], s["lsem1"], "dp", p)
+            wait_all(s["lrecv"], n_dp - 1, s["lsem0"], s["lsem1"], "dp")
+            s["lrecv"][md] = s["ltile"][...]
+            lsum = s["lrecv"][0]
+            for i in range(1, n_dp):
+                lsum = lsum + s["lrecv"][i]
+            gap = s["grad"][...] - resid
+            param_start(t + 1, [
+                lsum[0:1, 0:1] + DAMPING * _tile_sum(direction * direction),
+                _tile_sum(sol * gap),
+                lsum[1:2, 0:1] + DAMPING * _tile_sum(sol * direction),
+                _tile_sum(direction * gap),
+            ])
+            curv, x_gap, x_img, p_gap = param_finish(t + 1, 4)
+            alpha = rr / curv
+            x_new = sol + alpha * direction
+            shs = x_gap + alpha * (x_img + p_gap) + alpha * alpha * curv
+            s["x"][...] = x_new
+            blk = step_out.shape[0]
+            step_out[...] = s["x"][pl.ds(pl.multiple_of(md * blk, 8), blk)] * jnp.sqrt(D * UNITS / shs)
+            reach = jnp.sqrt(2.0 * TRIAL_KL / shs)
+            s["pb"][...] = (reach * x_new).astype(jnp.bfloat16)
+            continue
         image = dp_allreduce(t + 1)[...] + DAMPING * direction
         if t + 1 < iters:
             curv, r_img, img_img = param_round(
@@ -268,21 +318,6 @@
             s["p"][...] = p_new
             s["pb"][...] = p_new.astype(jnp.bfloat16)
             rr = rr_next
-        else:
-            sol = s["x"][...]
-            gap = s["grad"][...] - resid
-            curv, x_gap, x_img, p_gap = param_round(
-                t + 1,
-                [_tile_sum(direction * image), _tile_sum(sol * gap), _tile_sum(sol * image), _tile_sum(direction * gap)],
-            )
-            alpha = rr / curv
-            x_new = sol + alpha * direction
-            shs = x_gap + alpha * (x_img + p_gap) + alpha * alpha * curv
-            s["x"][...] = x_new
-            blk = step_out.shape[0]
-            step_out[...] = s["x"][pl.ds(pl.multiple_of(md * blk, 8), blk)] * jnp.sqrt(D * UNITS / shs)
-            reach = jnp.sqrt(2.0 * TRIAL_KL / shs)
-            s["pb"][...] = (reach * x_new).astype(jnp.bfloat16)
     last = iters + 1
     expand_head(s["pb"], s["chg"], shift_vals, last)
     head_allreduce(last)

time: 280 us -> 231 us (0.82)
  Pallas kernels: 269 us -> 221 us
    pallas_call x1, Pallas kernels: 269 us -> 221 us  [shards(): pl.pallas_call(functools.partial(_mega_kernel, names, dp_count, param_cou...]
where the time goes in v7:
time: 231 us
  Pallas kernels  221 us (96%)
  local copies, waits for them, and re-layouts  6.53 us (3%)
    pallas_call x1, Pallas kernels, shards(): pl.pallas_call(functools.partial(_mega_kernel, names, dp_count, param_cou...  221 us

profile of v7, /device:TPU:1, one launch (start us, length us, event | category | flops | bytes accessed | tf_op | source)
XLA Modules:
  0.0 230.6 jit_solution(13474197760380006362)
XLA Ops:
  0.6 0.7 multiply_exponential_fusion
  1.3 1.3 pad_convert_fusion
  2.6 0.8 pad.20.refs_7_
  3.4 1.6 pad.17.refs_4_
  5.0 1.6 pad.18.refs_5_
  6.6 221.5 %trust_region_step.1 = (f32[64,128]{1,0:T(8,128)}, f32[8,128]{1,0:T(8,128)}) custom-call(bf16[1024,2048]{1,0:T(8,128)(2,1)} %refs_0_.1, bf16[2048,128]{1,0:T(8,128)(2,1)} %refs_1_.1, bf16[48,128]{1,0:T(8,128)(2,1)} %get-tuple-element.7.refs_2_, f32[48,128]{1,0:T(8,128)} %get-tuple-element.6.refs_3_, f32[48,1024]{1,0:T(8,128)} %pad.17.refs_4_, ...), custom_call_target="tpu_custom_call" | custom-call | tf_op jit(solution)/shard_map/trust_region_step/pallas_call | solution.py:356
  228.0 1.2 slice.3
  229.2 1.4 copy.10
  (1 shorter events, 0.0 us)

commit v8 on v7

--- a/solution.py
+++ b/solution.py
@@ -42,6 +42,7 @@
         ("gb", pltpu.VMEM((rows, units), bf16)),
         ("chg", pltpu.VMEM((rows, units), f32)),
         ("part", pltpu.VMEM((width, units), f32)),
+        ("featT", pltpu.VMEM((width, rows), bf16)),
         ("grad", pltpu.VMEM((width, units), f32)),
         ("x", pltpu.VMEM((width, units), f32)),
         ("r", pltpu.VMEM((width, units), f32)),
@@ -219,8 +220,8 @@
         blk = max(cdp, min(256, width))
         for b in range(width // blk):
             c0 = b * blk
-            part[pl.ds(c0, blk), :] = lax.dot_general(
-                feat[:, pl.ds(c0, blk)], g[...], (((0,), (0,)), ((), ())), preferred_element_type=jnp.float32
+            part[pl.ds(c0, blk), :] = jnp.dot(
+                s["featT"][pl.ds(c0, blk), :], g[...], preferred_element_type=jnp.float32
             )
             if d is None:
                 continue
@@ -252,6 +253,9 @@
         moved = jnp.tanh(s["pre"][pl.ds(r0, blk), :] + s["chg"][pl.ds(r0, blk), :])
         return (moved - s["hid"][pl.ds(r0, blk), :]).astype(jnp.bfloat16)
 
+    tblk = min(256, width)
+    for c in range(width // tblk):
+        s["featT"][pl.ds(c * tblk, tblk), :] = feat[:, pl.ds(c * tblk, tblk)].T
     expand_head(wh, s["pre"], hidden_vals, 0, entry=True)
     head_allreduce(0)
     meanT = bmT[...] + s["hgat0"][...]

time: 231 us -> 230 us (level)
  no operation moved by 1% of the time
where the time goes in v8:
time: 230 us
  Pallas kernels  221 us (96%)
  local copies, waits for them, and re-layouts  6.53 us (3%)
    pallas_call x1, Pallas kernels, shards(): pl.pallas_call(functools.partial(_mega_kernel, names, dp_count, param_cou...  221 us

profile of v8, /device:TPU:1, one launch (start us, length us, event | category | flops | bytes accessed | tf_op | source)
XLA Modules:
  0.0 229.8 jit_solution(14600410164648168952)
XLA Ops:
  0.6 0.7 multiply_exponential_fusion
  1.3 1.3 pad_convert_fusion
  2.6 0.8 pad.20.refs_7_
  3.4 1.6 pad.17.refs_4_
  5.0 1.6 pad.18.refs_5_
  6.6 220.7 %trust_region_step.1 = (f32[64,128]{1,0:T(8,128)}, f32[8,128]{1,0:T(8,128)}) custom-call(bf16[1024,2048]{1,0:T(8,128)(2,1)} %refs_0_.1, bf16[2048,128]{1,0:T(8,128)(2,1)} %refs_1_.1, bf16[48,128]{1,0:T(8,128)(2,1)} %get-tuple-element.7.refs_2_, f32[48,128]{1,0:T(8,128)} %get-tuple-element.6.refs_3_, f32[48,1024]{1,0:T(8,128)} %pad.17.refs_4_, ...), custom_call_target="tpu_custom_call" | custom-call | tf_op jit(solution)/shard_map/trust_region_step/pallas_call | solution.py:360
  227.2 1.2 slice.3
  228.4 1.4 copy.10
  (1 shorter events, 0.0 us)

commit v9 on v8

--- a/solution.py
+++ b/solution.py
@@ -60,7 +60,7 @@
             (f"drecv{d}", pltpu.VMEM((n_dp, width // n_dp, units), f32)),
             (f"dgat{d}", pltpu.VMEM((width, units), f32)),
         ] + [(f"dsem{d}_{i}", dma) for i in range(4)]
-    for k in range(iters + 1):
+    for k in range(iters + 2):
         plan += [
             (f"stile{k}", pltpu.VMEM((8, 128), f32)),
             (f"srecv{k}", pltpu.VMEM((n_pa, 8, 128), f32)),
@@ -324,10 +324,15 @@
             rr = rr_next
     last = iters + 1
     expand_head(s["pb"], s["chg"], shift_vals, last)
-    head_allreduce(last)
-    dmeanT = s[f"hgat{last}"][...]
+    loc, recv = s[f"hloc{last}"], s[f"hrecv{last}"]
+    wait_all(recv, n_pa - 1, s[f"hsem{last}_0"], s[f"hsem{last}_1"], "param")
+    recv[mp] = hchunk(loc, mp)[...]
+    acc = recv[0]
+    for i in range(1, n_pa):
+        acc = acc + recv[i]
+    (kpart,) = param_round(iters + 1, [_tile_sum(acc * acc * hchunk(ivT, mp)[...])])
     ktile, krecv = s["ktile"], s["krecv"]
-    ktile[...] = jnp.broadcast_to(_tile_sum(dmeanT * dmeanT * ivT[...]), (8, 128))
+    ktile[...] = jnp.broadcast_to(kpart, (8, 128))
     for p in dpeers:
         send(ktile, krecv.at[md], s["ksem0"], s["ksem1"], "dp", p)
     wait_all(krecv, n_dp - 1, s["ksem0"], s["ksem1"], "dp")

time: 230 us -> 229 us (level)
  no operation moved by 1% of the time
where the time goes in v9:
time: 229 us
  Pallas kernels  219 us (96%)
  local copies, waits for them, and re-layouts  6.53 us (3%)
    pallas_call x1, Pallas kernels, shards(): pl.pallas_call(functools.partial(_mega_kernel, names, dp_count, param_cou...  219 us

profile of v9, /device:TPU:1, one launch (start us, length us, event | category | flops | bytes accessed | tf_op | source)
XLA Modules:
  0.0 228.6 jit_solution(17245840093202035969)
XLA Ops:
  0.6 0.7 multiply_exponential_fusion
  1.3 1.3 pad_convert_fusion
  2.6 0.8 pad.20.refs_7_
  3.4 1.6 pad.17.refs_4_
  5.0 1.6 pad.18.refs_5_
  6.6 219.4 %trust_region_step.1 = (f32[64,128]{1,0:T(8,128)}, f32[8,128]{1,0:T(8,128)}) custom-call(bf16[1024,2048]{1,0:T(8,128)(2,1)} %refs_0_.1, bf16[2048,128]{1,0:T(8,128)(2,1)} %refs_1_.1, bf16[48,128]{1,0:T(8,128)(2,1)} %get-tuple-element.7.refs_2_, f32[48,128]{1,0:T(8,128)} %get-tuple-element.6.refs_3_, f32[48,1024]{1,0:T(8,128)} %pad.17.refs_4_, ...), custom_call_target="tpu_custom_call" | custom-call | tf_op jit(solution)/shard_map/trust_region_step/pallas_call | solution.py:365
  226.0 1.2 slice.3
  227.2 1.4 copy.10
  (1 shorter events, 0.0 us)

commit v10 on v9

--- a/solution.py
+++ b/solution.py
@@ -88,8 +88,9 @@
     cdp = width // n_dp
     md = lax.axis_index("dp")
     mp = lax.axis_index("param")
-    dpeers = [lax.rem(md + j, n_dp) for j in range(1, n_dp)]
-    ppeers = [lax.rem(mp + j, n_pa) for j in range(1, n_pa)]
+    order = lambda n: sorted(range(1, n), key=lambda j: (min(j, n - j), j))
+    dpeers = [lax.rem(md + j, n_dp) for j in order(n_dp)]
+    ppeers = [lax.rem(mp + j, n_pa) for j in order(n_pa)]
 
     barrier = pltpu.get_barrier_semaphore()
     for p in dpeers:

time: 229 us -> 226 us (0.987)
    pallas_call x1, Pallas kernels: 219 us -> 217 us  [shards(): pl.pallas_call(functools.partial(_mega_kernel, names, dp_count, param_cou...]
where the time goes in v10:
time: 226 us
  Pallas kernels  217 us (96%)
  local copies, waits for them, and re-layouts  6.53 us (3%)
    pallas_call x1, Pallas kernels, shards(): pl.pallas_call(functools.partial(_mega_kernel, names, dp_count, param_cou...  217 us

profile of v10, /device:TPU:1, one launch (start us, length us, event | category | flops | bytes accessed | tf_op | source)
XLA Modules:
  0.0 225.9 jit_solution(2693445714439708855)
XLA Ops:
  0.6 0.7 multiply_exponential_fusion
  1.3 1.3 pad_convert_fusion
  2.6 0.8 pad.20.refs_7_
  3.4 1.6 pad.17.refs_4_
  5.0 1.6 pad.18.refs_5_
  6.6 216.8 %trust_region_step.1 = (f32[64,128]{1,0:T(8,128)}, f32[8,128]{1,0:T(8,128)}) custom-call(bf16[1024,2048]{1,0:T(8,128)(2,1)} %refs_0_.1, bf16[2048,128]{1,0:T(8,128)(2,1)} %refs_1_.1, bf16[48,128]{1,0:T(8,128)(2,1)} %get-tuple-element.7.refs_2_, f32[48,128]{1,0:T(8,128)} %get-tuple-element.6.refs_3_, f32[48,1024]{1,0:T(8,128)} %pad.17.refs_4_, ...), custom_call_target="tpu_custom_call" | custom-call | tf_op jit(solution)/shard_map/trust_region_step/pallas_call | solution.py:366
  223.4 1.2 slice.3
  224.6 1.4 copy.10
  (1 shorter events, 0.0 us)

commit v11 on v10

--- a/solution.py
+++ b/solution.py
@@ -195,8 +195,11 @@
             for p in ppeers:
                 send(tile, erecv.at[mp], es, er, "param", p)
         blk = max(lanes, 256)
-        for b in range(rows // blk):
-            r0 = b * blk
+        nb = rows // blk
+        per = blk // lanes
+        for b in range(nb):
+            bb = lax.rem(b + lax.rem(mp, groups) // per + 1, nb)
+            r0 = pl.multiple_of(bb * blk, blk)
             out[pl.ds(r0, blk), :] = jnp.dot(feat[pl.ds(r0, blk), :], vec_b[...], preferred_element_type=jnp.float32)
             vals = make_vals(r0, blk)
             loc[:, pl.ds(r0, blk)] = lax.dot_general(
@@ -204,9 +207,9 @@
             )
             if entry:
                 continue
-            for lg in range(r0 // lanes, (r0 + blk) // lanes):
+            for i in range(per):
                 for rg in range(ACT_PAD // HEAD_ROWS):
-                    k = rg * groups + lg
+                    k = rg * groups + bb * per + i
 
                     @pl.when(mp != k)
                     def _():
@@ -219,15 +222,19 @@
     def rowsum(g, d=None):
         part = s["part"]
         blk = max(cdp, min(256, width))
-        for b in range(width // blk):
-            c0 = b * blk
+        nb = width // blk
+        per = blk // cdp
+        for b in range(nb):
+            bb = lax.rem(b + md // per + 1, nb)
+            c0 = pl.multiple_of(bb * blk, blk)
             part[pl.ds(c0, blk), :] = jnp.dot(
                 s["featT"][pl.ds(c0, blk), :], g[...], preferred_element_type=jnp.float32
             )
             if d is None:
                 continue
             recv, sa, ra = s[f"drecv{d}"], s[f"dsem{d}_0"], s[f"dsem{d}_1"]
-            for k in range(c0 // cdp, (c0 + blk) // cdp):
+            for i in range(per):
+                k = bb * per + i
 
                 @pl.when(md != k)
                 def _():

time: 226 us -> 227 us (level)
  no operation moved by 1% of the time
where the time goes in v11:
time: 227 us
  Pallas kernels  218 us (96%)
  local copies, waits for them, and re-layouts  6.53 us (3%)
    pallas_call x1, Pallas kernels, shards(): pl.pallas_call(functools.partial(_mega_kernel, names, dp_count, param_cou...  218 us

profile of v11, /device:TPU:1, one launch (start us, length us, event | category | flops | bytes accessed | tf_op | source)
XLA Modules:
  0.0 226.8 jit_solution(13798492632371259317)
XLA Ops:
  0.6 0.7 multiply_exponential_fusion
  1.3 1.3 pad_convert_fusion
  2.6 0.8 pad.20.refs_7_
  3.4 1.6 pad.17.refs_4_
  5.0 1.6 pad.18.refs_5_
  6.6 217.6 %trust_region_step.1 = (f32[64,128]{1,0:T(8,128)}, f32[8,128]{1,0:T(8,128)}) custom-call(bf16[1024,2048]{1,0:T(8,128)(2,1)} %refs_0_.1, bf16[2048,128]{1,0:T(8,128)(2,1)} %refs_1_.1, bf16[48,128]{1,0:T(8,128)(2,1)} %get-tuple-element.7.refs_2_, f32[48,128]{1,0:T(8,128)} %get-tuple-element.6.refs_3_, f32[48,1024]{1,0:T(8,128)} %pad.17.refs_4_, ...), custom_call_target="tpu_custom_call" | custom-call | tf_op jit(solution)/shard_map/trust_region_step/pallas_call | solution.py:373
  224.2 1.2 slice.3
  225.4 1.4 copy.10
  (1 shorter events, 0.0 us)

commit v12 on v10

--- a/solution.py
+++ b/solution.py
@@ -36,6 +36,8 @@
     lanes = rows // groups
     dma = pltpu.SemaphoreType.DMA(())
     plan = [
+        ("fvm", pltpu.VMEM((rows, width), bf16)),
+        ("fsem", dma),
         ("pre", pltpu.VMEM((rows, units), f32)),
         ("hid", pltpu.VMEM((rows, units), f32)),
         ("slope", pltpu.VMEM((rows, units), f32)),
@@ -79,8 +81,9 @@
 
 
 def _mega_kernel(names, n_dp, n_pa, iters, batch, *refs):
-    (feat, wh, whtb, whtf, bmT, actT, adv, ivT, step_out, kl_out) = refs[:10]
+    (feat_hbm, wh, whtb, whtf, bmT, actT, adv, ivT, step_out, kl_out) = refs[:10]
     s = dict(zip(names, refs[10:]))
+    feat = s["fvm"]
     rows, width = feat.shape
     units = wh.shape[1]
     groups = n_pa // (ACT_PAD // HEAD_ROWS)
@@ -97,6 +100,9 @@
         pl.semaphore_signal(barrier, inc=1, device_id=_device("dp", p), device_id_type=MESH)
     for p in ppeers:
         pl.semaphore_signal(barrier, inc=1, device_id=_device("param", p), device_id_type=MESH)
+    fcopy = pltpu.make_async_copy(feat_hbm, feat, s["fsem"])
+    fcopy.start()
+    fcopy.wait()
 
     def wait_all(buf, count, send_sem, recv_sem, axis):
         cp = pltpu.make_async_remote_copy(
@@ -366,7 +372,7 @@
     step_unit, kl_tile = pl.pallas_call(
         functools.partial(_mega_kernel, names, dp_count, param_count, ITERS, batch),
         out_shape=(jax.ShapeDtypeStruct((block, units), jnp.float32), jax.ShapeDtypeStruct((8, 128), jnp.float32)),
-        in_specs=[vspec] * 8,
+        in_specs=[pl.BlockSpec(memory_space=pl.ANY)] + [vspec] * 7,
         out_specs=(vspec, vspec),
         scratch_shapes=[spec for _, spec in plan],
         compiler_params=pltpu.CompilerParams(collective_id=0, has_side_effects=True, vmem_limit_bytes=60 * 1024 * 1024),

time: 226 us -> 225 us (level)
  no operation moved by 1% of the time
where the time goes in v12:
time: 225 us; the launch traced here: 224 us
  Pallas kernels  215 us (96%)
  local copies, waits for them, and re-layouts  6.53 us (3%)
    pallas_call x1, Pallas kernels, shards(): pl.pallas_call(functools.partial(_mega_kernel, names, dp_count, param_cou...  215 us

profile of v12, /device:TPU:1, one launch (start us, length us, event | category | flops | bytes accessed | tf_op | source)
XLA Modules:
  0.0 224.4 jit_solution(15098595214896296314)
XLA Ops:
  0.6 0.7 multiply_exponential_fusion
  1.3 1.3 pad_convert_fusion
  2.6 0.8 pad.20.refs_7_
  3.4 1.6 pad.17.refs_4_
  5.0 1.6 pad.18.refs_5_
  6.6 215.2 %trust_region_step.1 = (f32[64,128]{1,0:T(8,128)}, f32[8,128]{1,0:T(8,128)}) custom-call(bf16[1024,2048]{1,0:T(8,128)(2,1)} %refs_0_.1, bf16[2048,128]{1,0:T(8,128)(2,1)} %refs_1_.1, bf16[48,128]{1,0:T(8,128)(2,1)} %get-tuple-element.7.refs_2_, f32[48,128]{1,0:T(8,128)} %get-tuple-element.6.refs_3_, f32[48,1024]{1,0:T(8,128)} %pad.17.refs_4_, ...), custom_call_target="tpu_custom_call" | custom-call | tf_op jit(solution)/shard_map/trust_region_step/pallas_call | solution.py:372
  221.8 1.2 slice.3
  223.0 1.4 copy.10
  (1 shorter events, 0.0 us)
